TPU v7x, 256 devices: a whole 4x4x8 slice. The times are simulated.
256 devices in a mesh: seq: 16 (over z, core), dp: 16 (over y, x).
Axes of the slice: x: 4, y: 4, z: 8, core: 2. Of those that a mesh axis runs over, the one named last changes fastest.
Arguments:
- queries: bfloat16 [16, 2048, 1280], P('dp', 'seq'), may hold values from -43 to 43
- key_rows: bfloat16 [16, 2048, 1280], P('dp', 'seq'), may hold values from -7 to 7
- value_rows: bfloat16 [16, 2048, 1280], P('dp', 'seq'), may hold values from -6 to 6
- resid_in: bfloat16 [16, 2048, 1280], P('dp', 'seq'), may hold values from -6 to 6
- llm_grad: bfloat16 [16, 3072, 1280], P('dp', 'seq'), may hold values from -6 to 6
- vision_slot: int32 [16, 3072], P('dp', 'seq'), may hold values from -1 to 2047, as said below
- window_mask: int32 [16, 32, 2], P('dp', 'seq'), may hold values from 0 to 1, as said below
- w_up: bfloat16 [1280, 2560], P('dp'), may hold values from -0.15625 to 0.15625
- w_down: bfloat16 [2560, 1280], P('dp'), may hold values from -0.125 to 0.125
- norm_gain: bfloat16 [1280], P('dp'), may hold values from 0.25 to 1.75
Outputs:
- grad_query: bfloat16 [16, 2048, 1280], P('dp', 'seq')
- grad_key: bfloat16 [16, 2048, 1280], P('dp', 'seq')
- grad_value: bfloat16 [16, 2048, 1280], P('dp', 'seq')
- grad_resid: bfloat16 [16, 2048, 1280], P('dp', 'seq')
- grad_up: bfloat16 [1280, 2560], P('seq', 'dp')
- grad_down: bfloat16 [2560, 1280], P('seq', 'dp')
- grad_gain: float32 [1280], replicated
Inputs may be any that keep to these rules, and one draw needn't show every extreme that they name: `vision_slot`: -1 marks a text position; every vision token of a batch stands at exactly one position. Positions come in aligned runs of 16: each run is text or the 16 consecutive vision tokens of one tile, in order. Each language-model shard holds exactly 8 tiles, and at most 32 vision tokens of one owner; in every batch, for every owner, some shard holds exactly 32 of that owner's vision tokens. `window_mask`: each owner's 2 blocks are split into images of one or more consecutive blocks; a block attends to exactly the blocks of its own image, itself included (entry i % 2 of row i is 1).
All inputs are finite; a program needn't handle non-finite values.
Results may differ from a plain program's by a relative error of at most 0.023.
Values may be sent and summed in bfloat16 or wider, within the bound.
A program may use at most 128 MiB of HBM per device.

v0:
```python
import math

import jax
import jax.numpy as jnp
from jax import lax
from jax.sharding import PartitionSpec as P

HEADS = 16
HDIM = 80
BLK = 64
PIECE = 16


def contract(left, right, left_dim, right_dim):
    return lax.dot_general(
        left, right, (((left_dim,), (right_dim,)), ((), ())), preferred_element_type=jnp.float32
    )


def per_device(
    queries,
    key_rows,
    value_rows,
    resid_in,
    llm_grad,
    vision_slot,
    window_mask,
    w_up,
    w_down,
    norm_gain,
):
    seq_count = lax.axis_size("seq")
    data_count = lax.axis_size("dp")
    query = queries[0]
    key_block = key_rows[0]
    value_block = value_rows[0]
    tokens, feat_dim = query.shape
    att_scale = 1.0 / math.sqrt(HDIM)
    up_full, down_full, gain_full = (
        lax.all_gather(w_up, "dp", axis=0, tiled=True),
        lax.all_gather(w_down, "dp", axis=0, tiled=True),
        lax.all_gather(norm_gain, "dp", axis=0, tiled=True),
    )
    slot_ids = vision_slot[0]
    piece_count = tokens // PIECE
    capacity = PIECE * (1 + (piece_count + seq_count - 2) // seq_count)
    owner_of = jnp.where(slot_ids >= 0, slot_ids // tokens, seq_count)
    onehot = (owner_of[:, None] == jnp.arange(seq_count)[None, :]).astype(jnp.int32)
    ranking = jnp.sum((jnp.cumsum(onehot, axis=0) - 1) * onehot, axis=1)
    target = jnp.where(slot_ids >= 0, owner_of * capacity + ranking, seq_count * capacity)
    send_rows = (
        jnp.zeros((seq_count * capacity, feat_dim), jnp.bfloat16)
        .at[target]
        .set(llm_grad[0], mode="drop")
    )
    send_ids = (
        jnp.full((seq_count * capacity,), -1, jnp.int32)
        .at[target]
        .set(jnp.where(slot_ids >= 0, slot_ids % tokens, -1), mode="drop")
    )
    recv_rows = lax.all_to_all(
        send_rows.reshape(seq_count, capacity, feat_dim),
        "seq",
        split_axis=0,
        concat_axis=0,
        tiled=True,
    )
    recv_ids = lax.all_to_all(
        send_ids.reshape(seq_count, capacity), "seq", split_axis=0, concat_axis=0, tiled=True
    )
    flat_ids = recv_ids.reshape(seq_count * capacity)
    landing = jnp.where(flat_ids >= 0, flat_ids, tokens)
    grad_rows = (
        jnp.zeros((tokens, feat_dim), jnp.bfloat16)
        .at[landing]
        .set(recv_rows.reshape(seq_count * capacity, feat_dim), mode="drop")
    )
    allowed = jnp.repeat(jnp.repeat(window_mask[0] > 0, BLK, axis=0), BLK, axis=1)
    q_heads = query.reshape(tokens, HEADS, HDIM)
    k_heads = key_block.reshape(tokens, HEADS, HDIM)
    v_heads = value_block.reshape(tokens, HEADS, HDIM)
    scores = (
        jnp.einsum("qhd,khd->hqk", q_heads, k_heads, preferred_element_type=jnp.float32) * att_scale
    )
    masked = jnp.where(allowed[None], scores, -jnp.inf)
    highest = jnp.max(masked, axis=2, keepdims=True)
    exp_terms = jnp.where(allowed[None], jnp.exp(masked - highest), 0.0)
    attn_probs = exp_terms / jnp.sum(exp_terms, axis=2, keepdims=True)
    probs_low = attn_probs.astype(jnp.bfloat16)
    attn_heads = jnp.einsum(
        "hqk,khd->qhd", probs_low, v_heads, preferred_element_type=jnp.float32
    ).astype(jnp.bfloat16)
    attn_out = attn_heads.reshape(tokens, feat_dim)
    hidden = resid_in[0].astype(jnp.float32) + attn_out.astype(jnp.float32)
    center = jnp.mean(hidden, axis=1, keepdims=True)
    variance = jnp.mean(jnp.square(hidden - center), axis=1, keepdims=True)
    inverse = lax.rsqrt(variance + 1e-06)
    normal_unit = (hidden - center) * inverse
    gain_wide = gain_full.astype(jnp.float32)
    normed = (normal_unit * gain_wide).astype(jnp.bfloat16)
    pre_act = jnp.dot(normed, up_full, preferred_element_type=jnp.float32)
    sig_gate = jax.nn.sigmoid(1.702 * pre_act)
    act_low = (pre_act * sig_gate).astype(jnp.bfloat16)
    down_term = contract(act_low, grad_rows, 0, 0)
    d_act = contract(grad_rows, down_full, 1, 1)
    d_pre = (d_act * (sig_gate + 1.702 * pre_act * sig_gate * (1.0 - sig_gate))).astype(
        jnp.bfloat16
    )
    d_normed = contract(d_pre, up_full, 1, 1)
    gain_term = jnp.sum(d_normed * normal_unit, axis=0)
    d_unit = d_normed * gain_wide
    d_hidden = inverse * (
        d_unit
        - jnp.mean(d_unit, axis=1, keepdims=True)
        - normal_unit * jnp.mean(d_unit * normal_unit, axis=1, keepdims=True)
    )
    grad_resid = (grad_rows.astype(jnp.float32) + d_hidden).astype(jnp.bfloat16)
    up_term = contract(normed, d_pre, 0, 0)
    grad_heads = grad_resid.reshape(tokens, HEADS, HDIM)
    grad_value = jnp.einsum(
        "hqk,qhd->khd", probs_low, grad_heads, preferred_element_type=jnp.float32
    ).astype(jnp.bfloat16)
    d_probs = jnp.einsum("qhd,khd->hqk", grad_heads, v_heads, preferred_element_type=jnp.float32)
    delta = jnp.einsum("qhd,qhd->hq", grad_heads, attn_heads, preferred_element_type=jnp.float32)
    d_scores = (attn_probs * (d_probs - delta[:, :, None]) * att_scale).astype(jnp.bfloat16)
    grad_query = jnp.einsum(
        "hqk,khd->qhd", d_scores, k_heads, preferred_element_type=jnp.float32
    ).astype(jnp.bfloat16)
    grad_key = jnp.einsum(
        "hqk,qhd->khd", d_scores, q_heads, preferred_element_type=jnp.float32
    ).astype(jnp.bfloat16)
    up_part, down_part = (
        lax.psum_scatter(
            up_term.astype(jnp.bfloat16), "seq", scatter_dimension=0, tiled=True
        ).astype(jnp.float32),
        lax.psum_scatter(
            down_term.astype(jnp.bfloat16), "seq", scatter_dimension=0, tiled=True
        ).astype(jnp.float32),
    )
    up_panel, down_panel = (
        lax.psum_scatter(
            up_part.astype(jnp.bfloat16), "dp", scatter_dimension=1, tiled=True
        ).astype(jnp.float32),
        lax.psum_scatter(
            down_part.astype(jnp.bfloat16), "dp", scatter_dimension=1, tiled=True
        ).astype(jnp.float32),
    )
    factor = 1.0 / math.sqrt(data_count * seq_count * tokens)
    gain_total = lax.psum(gain_term, ("seq", "dp"))
    return (
        grad_query.reshape(1, tokens, feat_dim),
        grad_key.reshape(1, tokens, feat_dim),
        grad_value.reshape(1, tokens, feat_dim),
        grad_resid[None],
        (up_panel * factor).astype(jnp.bfloat16),
        (down_panel * factor).astype(jnp.bfloat16),
        gain_total * factor,
    )


def solution(mesh):
    in_specs = (
        P("dp", "seq", None),
        P("dp", "seq", None),
        P("dp", "seq", None),
        P("dp", "seq", None),
        P("dp", "seq", None),
        P("dp", "seq"),
        P("dp", "seq", None),
        P("dp", None),
        P("dp", None),
        P("dp"),
    )
    out_specs = (
        P("dp", "seq", None),
        P("dp", "seq", None),
        P("dp", "seq", None),
        P("dp", "seq", None),
        P("seq", "dp"),
        P("seq", "dp"),
        P(),
    )
    return jax.shard_map(
        per_device, mesh=mesh, in_specs=in_specs, out_specs=out_specs, check_vma=False
    )
```

profile of v0, /device:TPU:31, one launch (start us, length us, event | category | flops | bytes accessed | tf_op | source)
XLA Modules:
  0.0 462.8 jit_solution(10220901300629912734)
XLA Ops:
  11.0 1.2 scatter_custom_fusion
  12.9 9.2 %all-to-all-start = ((s32[16,1,32]{2,1,0:T(1,128)}), s32[16,1,32]{2,1,0:T(1,128)S(1)}, u32[]{:S(2)}, u32[]{:S(2)}) async-start(s32[16,1,32]{2,1,0:T(1,128)} %all_to_all.9), calls=%async_computation | async-start | bytes 16384 | tf_op jit(solution)/shard_map/all_to_all | solution.py:68
  22.0 2.7 scatter_custom_fusion.1
  24.7 4.3 all-to-all-done
  29.0 4.3 all-to-all-start.1
  34.8 1.5 fusion.35
  36.3 1.5 convolution_convert_fusion.3
  40.8 30.2 %all-reduce.1 = bf16[1280]{0:T(1024)(128)(2,1)S(1)} all-reduce(bf16[1280]{0:T(1024)(128)(2,1)S(1)} %dynamic-update-slice), channel_id=1, replica_groups=mesh['seq'=16,'dp'=16] {'dp'}, use_global_device_ids=true, to_apply=%add.1 | all-reduce | flops 1280 | bytes 5120
  72.7 2.9 scatter_custom_fusion.2
  75.6 3.4 all-gather.5.cloned.1.call-done
  79.0 3.9 fusion.31
  83.0 65.6 %all-gather.3.cloned.1.call-done = bf16[2560,1280]{1,0:T(8,128)(2,1)} async-done(((bf16[160,1280]{1,0:T(8,128)(2,1)}), bf16[2560,1280]{1,0:T(8,128)(2,1)}) %all-gather.3.cloned.1.call-update) | async-done | bytes 6553616 | tf_op jit(solution)/shard_map/all_gather | solution.py:41
  148.6 5.1 %fusion.1 = bf16[128,2560]{1,0:T(8,128)(2,1)S(1)} fusion(bf16[128,1280]{1,0:T(8,128)(2,1)S(1)} %scatter_custom_fusion.2, bf16[2560,1280]{1,0:T(8,128)(2,1)} %all-gather.3.cloned.1.call-done, f32[128,2560]{1,0:T(8,128)S(1)} %fusion.31), kind=kOutput, calls=%fused_computation.7 | convolution fusion | flops 842137600 | bytes 8847360 | tf_op jit(solution)/shard_map/dot_general | solution.py:15
  153.7 4.7 %convolution_convert_fusion.1 = bf16[1280,2560]{1,0:T(8,128)(2,1)} fusion(bf16[128,2560]{1,0:T(8,128)(2,1)S(1)} %fusion.1, f32[128,1280]{1,0:T(8,128)S(1)} %get-tuple-element.32, f32[1280]{0:T(1024)S(1)} %convert_element_type.92, f32[128]{0:T(128)S(1)} %add_rsqrt_fusion, f32[128]{0:T(128)S(1)} %broadcast_multiply_fusion.3), kind=kOutput, calls=%fused_computation.5 | convolution fusion | flops 842792960 | bytes 7870464 | tf_op jit(solution)/shard_map/dot_general | solution.py:15
  158.4 4.7 %convolution_convert_fusion = bf16[2560,1280]{1,0:T(8,128)(2,1)} fusion(bf16[128,1280]{1,0:T(8,128)(2,1)S(1)} %scatter_custom_fusion.2, f32[128,2560]{1,0:T(8,128)S(1)} %fusion.31), kind=kOutput, calls=%fused_computation.4 | convolution fusion | flops 844103680 | bytes 8192000 | tf_op jit(solution)/shard_map/dot_general | solution.py:15
  163.2 5.2 %multiply_reduce_fusion = (f32[1280]{0:T(1024)S(1)}, f32[128]{0:T(128)S(1)}, f32[128]{0:T(128)S(1)}, f32[128,1280]{1,0:T(8,128)S(1)}) fusion(f32[128,1280]{1,0:T(8,128)S(1)} %get-tuple-element.32, f32[128]{0:T(128)S(1)} %add_rsqrt_fusion, f32[128]{0:T(128)S(1)} %broadcast_multiply_fusion.3, f32[1280]{0:T(1024)S(1)} %convert_element_type.92, ...), kind=kOutput, calls=%fused_computation.26 | convolution fusion | flops 840169984 | bytes 8531968 | tf_op jit(solution)/shard_map/dot_general | solution.py:15
  168.3 56.4 %reduce-scatter.9.cloned.1.call-done = bf16[80,2560]{1,0:T(8,128)(2,1)} async-done(((bf16[1280,2560]{1,0:T(8,128)(2,1)}), bf16[80,2560]{1,0:T(8,128)(2,1)}) %reduce-scatter.9.cloned.1.call-update) | async-done | bytes 409616 | tf_op jit(solution)/shard_map/reduce_scatter | solution.py:133
  224.8 2.1 copy.80
  228.0 1.7 fusion.8
  230.0 63.2 %reduce-scatter.11.cloned.1.call-done = bf16[160,1280]{1,0:T(8,128)(2,1)} async-done(((bf16[2560,1280]{1,0:T(8,128)(2,1)}), bf16[160,1280]{1,0:T(8,128)(2,1)}) %reduce-scatter.11.cloned.1.call-update) | async-done | bytes 409616 | tf_op jit(solution)/shard_map/reduce_scatter | solution.py:136
  293.2 2.1 copy.82
  295.9 0.9 copy.64
  299.1 77.3 %psum.7 = f32[1280]{0:T(1024)S(1)} all-reduce(f32[1280]{0:T(1024)S(1)} %get-tuple-element.28), channel_id=1, replica_groups=mesh['seq'=16,'dp'=16] {'seq','dp'}, use_global_device_ids=true, to_apply=%region_17.18 | all-reduce | flops 1280 | bytes 10240 | tf_op jit(solution)/shard_map/psum | solution.py:149
  378.5 76.0 %reduce-scatter.15.cloned.1.call-done = bf16[80,160]{1,0:T(8,128)(2,1)} async-done(((bf16[1280,160]{1,0:T(8,128)(2,1)}), bf16[80,160]{1,0:T(8,128)(2,1)}) %reduce-scatter.15.cloned.1.call-update) | async-done | bytes 25616
  (97 shorter events, 17.7 us)
Async XLA Ops:
  7.2 14.9 %copy-start = (bf16[1,192,1280]{2,1,0:T(8,128)(2,1)S(1)}, bf16[1,192,1280]{2,1,0:T(8,128)(2,1)}, u32[]{:S(2)}) copy-start(bf16[1,192,1280]{2,1,0:T(8,128)(2,1)} %param.14) | copy-start | bytes 1474564
  7.2 71.8 %all-gather.5.cloned.1.call-start = ((), (), s32[]{:S(2)}) async-start(), calls=%async_computation.7 | async-start | bytes 6963200 | tf_op jit(solution)/shard_map/all_gather | solution.py:40
  7.9 140.7 %all-gather.3.cloned.1.call-start = ((), (), s32[]{:S(2)}) async-start(), calls=%async_computation.6 | async-start | bytes 6963200 | tf_op jit(solution)/shard_map/all_gather | solution.py:41
  12.9 16.1 %all-to-all-start = ((s32[16,1,32]{2,1,0:T(1,128)}), s32[16,1,32]{2,1,0:T(1,128)S(1)}, u32[]{:S(2)}, u32[]{:S(2)}) async-start(s32[16,1,32]{2,1,0:T(1,128)} %all_to_all.9), calls=%async_computation | async-start | bytes 16384 | tf_op jit(solution)/shard_map/all_to_all | solution.py:68
  29.0 4.4 copy-start.8
  29.0 4.6 copy-start.9
  29.0 43.6 %all-to-all-start.1 = ((bf16[16,32,1280]{2,1,0:T(8,128)(2,1)}), bf16[16,32,1280]{2,1,0:T(8,128)(2,1)S(1)}, u32[]{:S(2)}, u32[]{:S(2)}) async-start(bf16[16,32,1280]{2,1,0:T(8,128)(2,1)} %bitcast.13), calls=%async_computation.1 | async-start | bytes 2621440 | tf_op jit(solution)/shard_map/all_to_all | solution.py:61
  33.3 1.0 copy-start.10
  33.3 1.2 copy-start.14
  33.3 191.5 %reduce-scatter.9.cloned.1.call-start = ((), (), s32[]{:S(2)}) async-start(), calls=%async_computation.8 | async-start | bytes 6963200 | tf_op jit(solution)/shard_map/reduce_scatter | solution.py:133
  33.6 2.7 copy-start.3
  34.3 2.0 copy-start.11
  34.5 1.8 copy-start.1
  38.6 1.9 copy-start.15
  38.7 32.3 %copy-start.13 = (bf16[1,128,1280]{2,1,0:T(8,128)(2,1)S(1)}, bf16[1,128,1280]{2,1,0:T(8,128)(2,1)}, u32[]{:S(2)}) copy-start(bf16[1,128,1280]{2,1,0:T(8,128)(2,1)} %param.13) | copy-start | bytes 983044
  158.4 134.9 %reduce-scatter.11.cloned.1.call-start = ((), (), s32[]{:S(2)}) async-start(), calls=%async_computation.9 | async-start | bytes 6963200 | tf_op jit(solution)/shard_map/reduce_scatter | solution.py:136
  163.1 213.8 %reduce-scatter.13.cloned.1.call-start = ((), (), s32[]{:S(2)}) async-start(), calls=%async_computation.10 | async-start | bytes 696320
  226.9 227.5 %reduce-scatter.15.cloned.1.call-start = ((), (), s32[]{:S(2)}) async-start(), calls=%async_computation.11 | async-start | bytes 696320
  226.9 1.0 copy-start.7
  226.9 1.1 copy-start.12
  227.3 2.4 copy-start.5
  228.0 1.7 copy-start.4
  229.7 65.6 %copy-start.2 = (bf16[1,128,1280]{1,2,0:T(8,128)(2,1)S(1)}, bf16[1,128,1280]{1,2,0:T(8,128)(2,1)}, u32[]{:S(2)}) copy-start(bf16[1,128,1280]{1,2,0:T(8,128)(2,1)} %copy-done.1) | copy-start | bytes 983044
  295.4 2.3 copy-start.17
  (2 other events, 1.4 us)
Sparse Core Ops, SparseCore 0:
  10.4 68.5 all-gather.4
  81.4 67.1 all-gather.2
  158.5 66.2 reduce-scatter.8
  227.2 65.9 reduce-scatter.10
  296.6 76.3 reduce-scatter.12
  376.3 78.0 reduce-scatter.14
where the time goes:
time: 467 us; the launch traced here: 463 us
  waiting for transfers between devices  270 us (58%)
  blocking collectives  107 us (23%)
  matrix products  29.5 us (6%)
  local copies, waits for them, and re-layouts  21 us (4%)
  between operations  15.1 us (3%)
  starting transfers between devices  13.7 us (3%)
  other arithmetic  5.58 us (1%)
    unnamed x8, waiting for transfers between devices  77.4 us
    psum x1, blocking collectives, per_device(): gain_total = lax.psum(gain_term, ('seq', 'dp'))  77.3 us
    all_gather x1, waiting for transfers between devices, per_device(): lax.all_gather(w_down, 'dp', axis=0, tiled=True)  65.6 us
    reduce_scatter x1, waiting for transfers between devices, per_device(): lax.psum_scatter(down_term.astype(jnp.bfloat16), 'seq', scatter_dimension...  63.2 us
    reduce_scatter x1, waiting for transfers between devices, per_device(): lax.psum_scatter(up_term.astype(jnp.bfloat16), 'seq', scatter_dimension=0...  56.4 us
    unnamed x1, blocking collectives  30.2 us
    dot_general x4, matrix products, contract(): lax.dot_general(left, right, (((left_dim,), (right_dim,)), ((), ())), pre...  19.6 us
    unnamed x49, local copies, waits for them, and re-layouts  12.1 us
  transfers between devices with their start and end apart: 8, of which 6 were waited for; matrix products, arithmetic and copies ran while one was open for 9% of the time, Pallas kernels for 0%

commit v1 on v0

v1 whole, which is shorter than its diff:
```python
import math

import jax
import jax.numpy as jnp
from jax import lax
from jax.experimental import pallas as pl
from jax.experimental.pallas import tpu as pltpu
from jax.sharding import PartitionSpec as P

HEADS = 16
HDIM = 80
BLK = 64
PIECE = 16
D = 1280
FF = 2560
TOK = 128
NS = 16
ND = 16
CAP = 32
NY, NX, NZ = 4, 4, 8
FQ = FF // NY
ROWS_DP = D // ND
FF_DP = FF // ND
WIN = 256
MESH = pl.DeviceIdType.MESH
BF = jnp.bfloat16
F32 = jnp.float32


def mm(left, right, left_dim, right_dim):
    return lax.dot_general(
        left, right, (((left_dim,), (right_dim,)), ((), ())), preferred_element_type=F32
    )


def window_start(z):
    return pl.multiple_of(128 * ((5 * z) // 4), 128)


def kernel(
    rows_ref,
    ids_ref,
    wup_ref,
    wdown_ref,
    unit_ref,
    gain_ref,
    dn_ref,
    grows_ref,
    gain_out_ref,
    ggain_ref,
    up_ref,
    down_ref,
    rr,
    ri,
    gr,
    wu,
    wd,
    ra,
    la,
    gate,
    dns,
    dnr,
    gt,
    cr,
    xs,
    xr,
    zs,
    zr,
    fs,
    fu,
    fd,
    gp,
    gs1,
    gp2,
    gs2,
    s_loc,
    s_rr,
    r_rr,
    s_ri,
    r_ri,
    s_gr,
    r_gr,
    s_wy,
    r_wy,
    s_wx,
    r_wx,
    s_rl,
    r_rl,
    s_na,
    r_na,
    s_ga,
    r_ga,
    s_dn,
    r_dn,
    s_c,
    r_c,
    s_x,
    r_x,
    s_z,
    r_z,
    s_f,
    r_f,
    s_g1,
    r_g1,
    s_g2,
    r_g2,
):
    s = lax.axis_index("seq")
    d = lax.axis_index("dp")
    z, c = s // 2, s % 2
    y, x = d // NX, d % NX

    def remote(src, dst, send, recv, to_s, to_d):
        return pltpu.make_async_remote_copy(
            src_ref=src,
            dst_ref=dst,
            send_sem=send,
            recv_sem=recv,
            device_id=(to_s, to_d),
            device_id_type=MESH,
        )

    def y_peer(k):
        return ((y + k) % NY) * NX + x

    def x_peer(k):
        return y * NX + (x + k) % NX

    barrier = pltpu.get_barrier_semaphore()
    for k in range(1, NS):
        pl.semaphore_signal(barrier, inc=1, device_id=((s + k) % NS, d), device_id_type=MESH)
    for k in range(1, ND):
        pl.semaphore_signal(barrier, inc=1, device_id=(s, (d + k) % ND), device_id_type=MESH)
    from_s = 2 * (d // 2) + 1
    own_final = jnp.logical_and(from_s == s, s == d)

    @pl.when(jnp.logical_not(own_final))
    def _():
        pl.semaphore_signal(barrier, inc=1, device_id=(from_s, s), device_id_type=MESH)

    pl.semaphore_wait(barrier, NS + ND - 2 + 2 * c - jnp.where(own_final, 1, 0))

    def gain_copy(k):
        return remote(gain_ref, gr.at[d], s_gr.at[k], r_gr.at[k], s, (d + k) % ND)

    for k in range(1, ND):
        gain_copy(k).start()

    def row_copy(k):
        to = (s + k) % NS
        return remote(rows_ref.at[to], rr.at[s], s_rr.at[k], r_rr.at[k], to, d)

    def id_copy(k):
        to = (s + k) % NS
        return remote(ids_ref.at[to], ri.at[s], s_ri.at[k], r_ri.at[k], to, d)

    for k in range(1, NS):
        id_copy(k).start()
        row_copy(k).start()
    own_rows = pltpu.make_async_copy(rows_ref.at[s], rr.at[s], s_loc.at[0])
    own_ids = pltpu.make_async_copy(ids_ref.at[s], ri.at[s], s_loc.at[1])
    own_rows.start()
    own_ids.start()

    def quarter(q):
        return wup_ref.at[:, pl.ds(pl.multiple_of(q * FQ, 128), FQ)]

    def wy_copy(k):
        return remote(
            quarter((y + k) % NY), wu.at[y, x], s_wy.at[k], r_wy.at[k], s, y_peer(k)
        )

    def ux_copy(k):
        return remote(wu.at[:, x], wu.at[:, x], s_wx.at[k], r_wx.at[k], s, x_peer(k))

    def dx_copy(k):
        return remote(wd.at[x], wd.at[x], s_wx.at[k], r_wx.at[k], s, x_peer(k))

    def ul_copy(k):
        at = (x + NX - k) % NX
        return remote(wu.at[:, at], wu.at[:, at], s_rl.at[k], r_rl.at[k], s + 1, d)

    def dl_copy(k):
        at = (x + NX - k) % NX
        return remote(wd.at[at], wd.at[at], s_rl.at[k], r_rl.at[k], s - 1, d)

    own_up = pltpu.make_async_copy(quarter(y), wu.at[y, x], s_loc.at[2])
    own_down = pltpu.make_async_copy(wdown_ref, wd.at[x], s_loc.at[3])

    @pl.when(c == 0)
    def _():
        for k in range(1, NY):
            wy_copy(k).start()
        own_up.start()
        own_up.wait()

    @pl.when(c == 1)
    def _():
        own_down.start()
        own_down.wait()
        for k in range(1, NX):
            dx_copy(k).start()
        dl_copy(0).start()

    gr[d] = gain_ref[...]
    for k in range(1, ND):
        gain_copy(k).wait_recv()
    gain_full = jnp.sum(gr[...], axis=0)
    gain_out_ref[...] = gain_full
    ra[0, y] = (unit_ref[...] * gain_full).astype(BF)

    def na_copy(k):
        return remote(ra.at[0, y], ra.at[0, y], s_na.at[k], r_na.at[k], s, y_peer(k))

    for k in range(1, NY):
        na_copy(k).start()

    @pl.when(c == 0)
    def _():
        for k in range(1, NY):
            wy_copy(k).wait_recv()
        for k in range(1, NX):
            ux_copy(k).start()
        ul_copy(0).start()
        for k in (1, 3, 2):
            ux_copy(k).wait_recv()
            ul_copy(k).start()
        for k in range(NX):
            dl_copy(k).wait_recv()

    @pl.when(c == 1)
    def _():
        for k in (1, 3, 2):
            dx_copy(k).wait_recv()
            dl_copy(k).start()
        for k in range(NX):
            ul_copy(k).wait_recv()

    for k in range(1, NY):
        na_copy(k).wait_recv()

    half = 2 * TOK

    def up_step(i, carry):
        rows = pl.ds(pl.multiple_of(i * half, half), half)
        pre = mm(
            ra[0, pl.ds(2 * i, 2)].reshape(half, D), wu[...].reshape(D, FQ), 1, 0
        )
        sig = jax.nn.sigmoid(1.702 * pre)
        la[1, rows, :] = (pre * sig).astype(BF)
        gate[rows, :] = sig + 1.702 * pre * sig * (1.0 - sig)
        return carry

    lax.fori_loop(0, 2, up_step, 0)

    own_rows.wait()
    own_ids.wait()
    for k in range(1, NS):
        id_copy(k).wait_recv()
        row_copy(k).wait_recv()
    total = None
    token = lax.broadcasted_iota(jnp.int32, (TOK, 128), 0)
    for j in range(4):
        ids = jnp.max(ri[4 * j : 4 * j + 4], axis=0)
        place = jnp.where(token == ids, 1.0, 0.0).astype(BF)
        part = mm(place, rr[4 * j : 4 * j + 4].reshape(4 * CAP, D), 1, 0)
        total = part if total is None else total + part
    own_grad = total.astype(BF)
    ra[1, y] = own_grad
    grows_ref[...] = own_grad

    def ga_copy(k):
        return remote(ra.at[1, y], ra.at[1, y], s_ga.at[k], r_ga.at[k], s, y_peer(k))

    for k in range(1, NY):
        ga_copy(k).start()
    for k in range(1, NY):
        ga_copy(k).wait_recv()

    def down_step(i, carry):
        rows = pl.ds(pl.multiple_of(i * half, half), half)
        d_act = mm(
            ra[1, pl.ds(2 * i, 2)].reshape(half, D), wd[...].reshape(FQ, D), 1, 1
        )
        la[0, rows, :] = (d_act * gate[rows, :]).astype(BF)
        return carry

    lax.fori_loop(0, 2, down_step, 0)

    def norm_step(i, acc):
        rows = pl.ds(pl.multiple_of(i * half, half), half)
        part = mm(la[0, rows, :], wu[...].reshape(D, FQ), 1, 1)
        dns[pl.ds(2 * i, 2)] = part.astype(BF).reshape(2, TOK, D)
        normed = ra[0, pl.ds(2 * i, 2)].reshape(half, D).astype(F32)
        return acc + jnp.sum(part * normed, axis=0, keepdims=True)

    gp[...] = lax.fori_loop(0, 2, norm_step, jnp.zeros((1, D), F32))

    def dn_copy(k):
        to = (y + k) % NY
        return remote(dns.at[to], dnr.at[y], s_dn.at[k], r_dn.at[k], s, to * NX + x)

    for k in range(1, NY):
        dn_copy(k).start()

    def g1_copy(k):
        return remote(gp, gs1.at[s], s_g1.at[k], r_g1.at[k], (s + k) % NS, d)

    for k in range(1, NS):
        g1_copy(k).start()

    def weight_grad(part):
        def step(i, carry):
            lanes = pl.ds(pl.multiple_of(i * 128, 128), 128)
            value = mm(la[part, :, lanes], ra[part].reshape(NY * TOK, D), 0, 0)
            gt[part, pl.ds(pl.multiple_of(i * 128, 128), 128), :] = value.astype(BF)
            return carry

        lax.fori_loop(0, FQ // 128, step, 0)

    c_copy = remote(gt.at[1 - c], cr, s_c.at[0], r_c.at[0], s + 1 - 2 * c, d)
    weight_grad(1 - c)
    c_copy.start()
    weight_grad(c)
    c_copy.wait_recv()

    def c_sum(i, carry):
        rows = pl.ds(pl.multiple_of(i * 32, 32), 32)
        xs[rows, :] = (gt[c, rows, :].astype(F32) + cr[rows, :].astype(F32)).astype(BF)
        return carry

    lax.fori_loop(0, FQ // 32, c_sum, 0)

    def block(i):
        return pl.ds(pl.multiple_of(i * FF_DP, FF_DP), FF_DP)

    def x_copy(k):
        to = (x + k) % NX
        return remote(xs.at[block(to)], xr.at[x], s_x.at[k], r_x.at[k], s, y * NX + to)

    for k in range(1, NX):
        x_copy(k).start()

    gs1[s] = gp[...]
    for k in range(1, NS):
        g1_copy(k).wait_recv()
    gp2[...] = jnp.sum(gs1[...], axis=0)

    def g2_copy(k):
        return remote(gp2, gs2.at[d], s_g2.at[k], r_g2.at[k], s, (d + k) % ND)

    for k in range(1, ND):
        g2_copy(k).start()

    dnr[y] = dns[y]
    for k in range(1, NY):
        dn_copy(k).wait_recv()

    def dn_sum(i, carry):
        rows = pl.ds(pl.multiple_of(i * 32, 32), 32)
        dn_ref[rows, :] = jnp.sum(dnr[:, rows, :].astype(F32), axis=0)
        return carry

    lax.fori_loop(0, TOK // 32, dn_sum, 0)

    for k in range(1, NX):
        x_copy(k).wait_recv()
    xr[x] = xs[block(x), :]

    def x_sum(i, carry):
        rows = pl.ds(pl.multiple_of(i * 32, 32), 32)
        zs[rows, :] = jnp.sum(xr[:, rows, :].astype(F32), axis=0).astype(BF)
        return carry

    lax.fori_loop(0, FF_DP // 32, x_sum, 0)

    def z_copy(k):
        to = (z + k) % NZ
        return remote(
            zs.at[:, pl.ds(window_start(to), WIN)],
            zr.at[z],
            s_z.at[k],
            r_z.at[k],
            2 * to + c,
            d,
        )

    for k in range(1, NZ):
        z_copy(k).start()
    zr[z] = zs[:, pl.ds(window_start(z), WIN)]

    gs2[d] = gp2[...]
    for k in range(1, ND):
        g2_copy(k).wait_recv()
    factor = 1.0 / math.sqrt(NS * ND * TOK)
    ggain_ref[...] = jnp.sum(gs2[...], axis=0) * factor / gain_out_ref[...]

    for k in range(1, NZ):
        z_copy(k).wait_recv()
    fs[...] = (jnp.sum(zr[...].astype(F32), axis=0) * factor).astype(BF)

    u_copy = remote(fs, fu, s_f.at[0], r_f.at[0], s + 1, d)
    d0_copy = remote(fs, fd, s_f.at[1], r_f.at[1], d, 2 * z)
    d1_copy = remote(fs, fd, s_f.at[2], r_f.at[1], d, 2 * z + 1)
    d_self = pltpu.make_async_copy(fs, fd, s_loc.at[4])

    @pl.when(c == 0)
    def _():
        u_copy.start()
        up_ref[...] = fs[...]

    @pl.when(c == 1)
    def _():
        d0_copy.start()

        @pl.when(s == d)
        def _():
            d_self.start()
            d_self.wait()

        @pl.when(s != d)
        def _():
            d1_copy.start()

        u_copy.wait_recv()
        up_ref[...] = fu[...]

    @pl.when(jnp.logical_not(own_final))
    def _():
        d0_copy.wait_recv()

    down_ref[...] = fd[...]

    @pl.when(c == 0)
    def _():
        u_copy.wait_send()
        for k in range(1, NY):
            wy_copy(k).wait_send()
        for k in range(1, NX):
            ux_copy(k).wait_send()
        for k in range(NX):
            ul_copy(k).wait_send()

    @pl.when(c == 1)
    def _():
        d0_copy.wait_send()

        @pl.when(s != d)
        def _():
            d1_copy.wait_send()

        for k in range(1, NX):
            dx_copy(k).wait_send()
        for k in range(NX):
            dl_copy(k).wait_send()

    c_copy.wait_send()
    for k in range(1, NS):
        row_copy(k).wait_send()
        id_copy(k).wait_send()
        g1_copy(k).wait_send()
    for k in range(1, ND):
        gain_copy(k).wait_send()
        g2_copy(k).wait_send()
    for k in range(1, NY):
        na_copy(k).wait_send()
        ga_copy(k).wait_send()
        dn_copy(k).wait_send()
    for k in range(1, NX):
        x_copy(k).wait_send()
    for k in range(1, NZ):
        z_copy(k).wait_send()


def exchange(rows, ids, w_up, w_down, unit, gain_placed):
    vm = pl.BlockSpec(memory_space=pltpu.VMEM)
    hbm = pl.BlockSpec(memory_space=pl.ANY)
    sem = pltpu.SemaphoreType.DMA
    pairs = [NS, NS, ND, NY, NX, NX, NY, NY, NY, 1, NX, NZ, 3, NS, ND]
    sems = [sem((5,))]
    for n in pairs:
        sems += [sem((n,)), sem((n,))]
    return pl.pallas_call(
        kernel,
        out_shape=(
            jax.ShapeDtypeStruct((TOK, D), F32),
            jax.ShapeDtypeStruct((TOK, D), BF),
            jax.ShapeDtypeStruct((1, D), F32),
            jax.ShapeDtypeStruct((1, D), F32),
            jax.ShapeDtypeStruct((FF_DP, WIN), BF),
            jax.ShapeDtypeStruct((FF_DP, WIN), BF),
        ),
        in_specs=[hbm, hbm, hbm, hbm, vm, vm],
        out_specs=(vm,) * 6,
        scratch_shapes=[
            pltpu.VMEM((NS, CAP, D), BF),
            pltpu.VMEM((NS, 1, 128), jnp.int32),
            pltpu.VMEM((ND, 1, D), F32),
            pltpu.VMEM((NY, NX, ROWS_DP, FQ), BF),
            pltpu.VMEM((NX, FF_DP, D), BF),
            pltpu.VMEM((2, NY, TOK, D), BF),
            pltpu.VMEM((2, NY * TOK, FQ), BF),
            pltpu.VMEM((NY * TOK, FQ), F32),
            pltpu.VMEM((NY, TOK, D), BF),
            pltpu.VMEM((NY, TOK, D), BF),
            pltpu.VMEM((2, FQ, D), BF),
            pltpu.VMEM((FQ, D), BF),
            pltpu.VMEM((FQ, D), BF),
            pltpu.VMEM((NX, FF_DP, D), BF),
            pltpu.VMEM((FF_DP, D), BF),
            pltpu.VMEM((NZ, FF_DP, WIN), BF),
            pltpu.VMEM((FF_DP, WIN), BF),
            pltpu.VMEM((FF_DP, WIN), BF),
            pltpu.VMEM((FF_DP, WIN), BF),
            pltpu.VMEM((1, D), F32),
            pltpu.VMEM((NS, 1, D), F32),
            pltpu.VMEM((1, D), F32),
            pltpu.VMEM((ND, 1, D), F32),
            *sems,
        ],
        compiler_params=pltpu.CompilerParams(
            collective_id=0, has_side_effects=True, vmem_limit_bytes=56 * 2**20
        ),
    )(rows, ids, w_up, w_down, unit, gain_placed)


def per_device(
    queries,
    key_rows,
    value_rows,
    resid_in,
    llm_grad,
    vision_slot,
    window_mask,
    w_up,
    w_down,
    norm_gain,
):
    s_at = lax.axis_index("seq")
    d_at = lax.axis_index("dp")
    query = queries[0]
    tokens, feat_dim = query.shape
    att_scale = 1.0 / math.sqrt(HDIM)

    slot_ids = vision_slot[0]
    n_pos = slot_ids.shape[0]
    owner = jnp.where(slot_ids >= 0, slot_ids // tokens, NS)
    before = jnp.arange(n_pos)[None, :] < jnp.arange(n_pos)[:, None]
    rank = jnp.sum(((owner[:, None] == owner[None, :]) & before).astype(jnp.int32), axis=1)
    target = jnp.where(slot_ids >= 0, owner * CAP + rank, -1)
    hit = jnp.arange(NS * CAP)[:, None] == target[None, :]
    send_rows = jnp.dot(hit.astype(BF), llm_grad[0], preferred_element_type=F32).astype(BF)
    landing = jnp.max(jnp.where(hit, (slot_ids % tokens)[None, :], -1), axis=1)
    lane = jnp.arange(128)
    send_ids = jnp.where(
        (lane // CAP == s_at % 4)[None, :], jnp.tile(landing.reshape(NS, CAP), (1, 4)), -1
    )

    allowed = jnp.repeat(jnp.repeat(window_mask[0] > 0, BLK, axis=0), BLK, axis=1)
    q_heads = query.reshape(tokens, HEADS, HDIM)
    k_heads = key_rows[0].reshape(tokens, HEADS, HDIM)
    v_heads = value_rows[0].reshape(tokens, HEADS, HDIM)
    scores = jnp.einsum("qhd,khd->hqk", q_heads, k_heads, preferred_element_type=F32) * att_scale
    masked = jnp.where(allowed[None], scores, -jnp.inf)
    highest = jnp.max(masked, axis=2, keepdims=True)
    exp_terms = jnp.where(allowed[None], jnp.exp(masked - highest), 0.0)
    attn_probs = exp_terms / jnp.sum(exp_terms, axis=2, keepdims=True)
    probs_low = attn_probs.astype(BF)
    attn_heads = jnp.einsum(
        "hqk,khd->qhd", probs_low, v_heads, preferred_element_type=F32
    ).astype(BF)
    attn_out = attn_heads.reshape(tokens, feat_dim)
    hidden = resid_in[0].astype(F32) + attn_out.astype(F32)
    center = jnp.mean(hidden, axis=1, keepdims=True)
    variance = jnp.mean(jnp.square(hidden - center), axis=1, keepdims=True)
    inverse = lax.rsqrt(variance + 1e-06)
    normal_unit = (hidden - center) * inverse

    mine = (jnp.arange(feat_dim) // ROWS_DP) == d_at
    gain_placed = jnp.where(mine, jnp.tile(norm_gain.astype(F32), ND), 0.0)[None, :]

    d_normed, grad_rows, gain_wide, grad_gain, up_win, down_win = exchange(
        send_rows.reshape(NS, CAP, feat_dim),
        send_ids.reshape(NS, 1, 128),
        w_up,
        w_down,
        normal_unit,
        gain_placed,
    )

    d_unit = d_normed * gain_wide
    d_hidden = inverse * (
        d_unit
        - jnp.mean(d_unit, axis=1, keepdims=True)
        - normal_unit * jnp.mean(d_unit * normal_unit, axis=1, keepdims=True)
    )
    grad_resid = (grad_rows.astype(F32) + d_hidden).astype(BF)
    grad_heads = grad_resid.reshape(tokens, HEADS, HDIM)
    grad_value = jnp.einsum(
        "hqk,qhd->khd", probs_low, grad_heads, preferred_element_type=F32
    ).astype(BF)
    d_probs = jnp.einsum("qhd,khd->hqk", grad_heads, v_heads, preferred_element_type=F32)
    delta = jnp.einsum("qhd,qhd->hq", grad_heads, attn_heads, preferred_element_type=F32)
    d_scores = (attn_probs * (d_probs - delta[:, :, None]) * att_scale).astype(BF)
    grad_query = jnp.einsum("hqk,khd->qhd", d_scores, k_heads, preferred_element_type=F32).astype(BF)
    grad_key = jnp.einsum("hqk,qhd->khd", d_scores, q_heads, preferred_element_type=F32).astype(BF)

    z_at = s_at // 2
    up_own = lax.dynamic_slice_in_dim(
        up_win, 32 * (z_at % 4) + ROWS_DP * (s_at % 2), ROWS_DP, axis=1
    ).T
    down_own = lax.dynamic_slice_in_dim(
        down_win, 32 * ((d_at // 2) % 4) + ROWS_DP * (d_at % 2), ROWS_DP, axis=1
    )
    return (
        grad_query.reshape(1, tokens, feat_dim),
        grad_key.reshape(1, tokens, feat_dim),
        grad_value.reshape(1, tokens, feat_dim),
        grad_resid[None],
        up_own,
        down_own,
        grad_gain.reshape(feat_dim),
    )


def solution(mesh):
    row3 = P("dp", "seq", None)
    in_specs = (
        row3,
        row3,
        row3,
        row3,
        row3,
        P("dp", "seq"),
        row3,
        P("dp", None),
        P("dp", None),
        P("dp"),
    )
    out_specs = (row3, row3, row3, row3, P("seq", "dp"), P("seq", "dp"), P())
    return jax.shard_map(
        per_device, mesh=mesh, in_specs=in_specs, out_specs=out_specs, check_vma=False
    )
```

time: 467 us -> 145 us (0.31)
  the two profiles are of different devices: /device:TPU:31 before, /device:TPU:32 now
where the time goes in v1:
time: 145 us
  Pallas kernels  117 us (81%)
  local copies, waits for them, and re-layouts  11.3 us (8%)
  other arithmetic  9.52 us (7%)
  matrix products  5.66 us (4%)
    pallas_call x1, Pallas kernels, exchange(): pl.pallas_call(kernel, out_shape=(jax.ShapeDtypeStruct((TOK, D), F32), ja...  117 us
    unnamed x29, local copies, waits for them, and re-layouts  8.08 us

profile of v1, /device:TPU:32, one launch (start us, length us, event | category | flops | bytes accessed | tf_op | source)
XLA Modules:
  0.0 144.8 jit_solution(16224953067604228973)
XLA Ops:
  0.8 0.7 compare_bitcast_fusion
  1.8 0.7 compare_select_fusion.6
  2.5 0.7 and_select_fusion.1
  3.1 0.7 compare_select_fusion.5
  4.0 0.7 compare_select_fusion.4
  4.9 0.7 tile.22
  5.7 0.6 compare_select_fusion.gain_ref
  6.4 0.6 broadcast_select_fusion.ids_ref
  7.0 1.2 copy.52
  8.2 1.2 copy.53
  10.2 1.0 copy-done.9
  11.8 0.7 copy-done.2
  12.9 1.0 subtract_multiply_fusion.unit_ref
  13.8 1.8 %convolution_convert_fusion = bf16[512,1280]{1,0:T(8,128)(2,1)} fusion(bf16[1,192,1280]{2,1,0:T(8,128)(2,1)S(1)} %copy-done, s32[192]{0:T(256)S(1)} %bitcast.77), kind=kOutput, calls=%fused_computation.1 | convolution fusion | flops 252411904 | bytes 1803008 | tf_op jit(solution)/shard_map/dot_general | solution.py:552
  15.6 117.3 %shard_map.153 = (f32[128,1280]{1,0:T(8,128)}, bf16[128,1280]{1,0:T(8,128)(2,1)}, f32[1,1280]{1,0:T(1,128)}, f32[1,1280]{1,0:T(1,128)}, bf16[160,256]{1,0:T(8,128)(2,1)}, /*index=5*/bf16[160,256]{1,0:T(8,128)(2,1)}) custom-call(bf16[16,32,1280]{2,1,0:T(8,128)(2,1)} %bitcast.60, s32[16,1,128]{2,1,0:T(1,128)} %broadcast_select_fusion.ids_ref, ...), custom_call_target="tpu_custom_call" | custom-call | tf_op jit(solution)/shard_map/pallas_call | solution.py:483
  133.0 0.8 reduce.1
  133.8 1.3 multiply_reduce_fusion.2
  135.8 0.6 reduce.2
  136.4 1.6 %dynamic-slice_bitcast_fusion = (bf16[80,160]{0,1:T(8,128)(2,1)S(1)}, bf16[160,80]{1,0:T(8,128)(2,1)}) fusion(bf16[160,256]{1,0:T(8,128)(2,1)S(1)} %copy-done.7, s32[]{:T(128)S(6)} %select_n.143, bf16[160,256]{1,0:T(8,128)(2,1)} %get-tuple-element.17, s32[]{:T(128)S(6)} %select_n.147), kind=kLoop, calls=%fused_computation.34 | loop fusion | bytes 102408 | tf_op jit(solution)/shard_map/transpose | solution.py:611
  138.0 0.7 copy.65
  139.0 1.7 %fusion.7 = bf16[16,128,128]{1,2,0:T(8,128)(2,1)S(1)} fusion(bf16[128,16,80]{0,2,1:T(8,128)(2,1)S(1)} %bitcast.68, bf16[128,16,80]{0,2,1:T(8,128)(2,1)S(1)} %bitcast.72, f32[16,128]{1,0:T(8,128)S(1)} %fusion.8, f32[16,128,128]{1,2,0:T(8,128)} %copy-done.9, f32[16,128]{1,0:T(8,128)S(1)} %get-tuple-element.44), kind=kOutput, calls=%fused_computation.10 | convolution fusion | flops 43253760 | bytes 2244608 | tf_op jit(solution)/shard_map/qhd,khd->hqk/dot_general | solution.py:602
  141.3 0.9 copy.64
  143.0 0.9 copy.62
  143.9 0.9 copy.63
  (47 shorter events, 4.9 us)
Async XLA Ops:
  0.6 13.2 %copy-start = (bf16[1,192,1280]{2,1,0:T(8,128)(2,1)S(1)}, bf16[1,192,1280]{2,1,0:T(8,128)(2,1)}, u32[]{:S(2)}) copy-start(bf16[1,192,1280]{2,1,0:T(8,128)(2,1)} %param.14) | copy-start | bytes 1474564
  0.6 8.7 %copy-start.5 = (bf16[1,128,1280]{2,1,0:T(8,128)(2,1)S(1)}, bf16[1,128,1280]{2,1,0:T(8,128)(2,1)}, u32[]{:S(2)}) copy-start(bf16[1,128,1280]{2,1,0:T(8,128)(2,1)} %param.12) | copy-start | bytes 983044
  10.2 1.0 copy-start.9
  11.5 1.0 copy-start.2
  15.6 118.1 %copy-start.1 = (f32[128,1280]{1,0:T(8,128)S(1)}, f32[128,1280]{1,0:T(8,128)}, u32[]{:S(2)}) copy-start(f32[128,1280]{1,0:T(8,128)} %subtract_multiply_fusion.unit_ref) | copy-start | bytes 1966084
  133.0 2.2 %copy-start.3 = (f32[128,1280]{1,0:T(8,128)S(1)}, f32[128,1280]{1,0:T(8,128)}, u32[]{:S(2)}) copy-start(f32[128,1280]{1,0:T(8,128)} %get-tuple-element.14) | copy-start | bytes 1966084
  133.8 1.4 copy-start.6
  135.1 0.7 copy-start.8
  135.1 1.3 copy-start.7
  135.4 5.4 %copy-start.4 = (bf16[128,1280]{1,0:T(8,128)(2,1)}, bf16[128,1280]{1,0:T(8,128)(2,1)S(1)}, u32[]{:S(2)}) copy-start(bf16[128,1280]{1,0:T(8,128)(2,1)S(1)} %add_convert_fusion) | copy-start | bytes 983044
  139.0 1.7 %copy-start.10 = (f32[16,128,128]{1,2,0:T(8,128)S(1)}, f32[16,128,128]{1,2,0:T(8,128)}, u32[]{:S(2)}) copy-start(f32[16,128,128]{1,2,0:T(8,128)} %copy-done.9) | copy-start | bytes 3145732

commit v2 on v1

v2 whole, which is shorter than its diff:
```python
import math

import jax
import jax.numpy as jnp
from jax import lax
from jax.experimental import pallas as pl
from jax.experimental.pallas import tpu as pltpu
from jax.sharding import PartitionSpec as P

HEADS = 16
HDIM = 80
BLK = 64
D = 1280
FF = 2560
TOK = 128
POS = 192
NS = 16
ND = 16
CAP = 32
NY, NX, NZ = 4, 4, 8
FQ = FF // NY
ROWS_DP = D // ND
FF_DP = FF // ND
WIN = 256
NP = 5
PW = D // NP
NR = 5
RW = FF_DP // NR
MESH = pl.DeviceIdType.MESH
BF = jnp.bfloat16
F32 = jnp.float32


def mm(left, right, left_dim, right_dim):
    return lax.dot_general(
        left, right, (((left_dim,), (right_dim,)), ((), ())), preferred_element_type=F32
    )


def iota(shape, dim):
    return lax.broadcasted_iota(jnp.int32, shape, dim)


def to_column(row):
    n = row.shape[1]
    same = iota((n, n), 0) == iota((n, n), 1)
    return jnp.sum(jnp.where(same, row, 0.0), axis=1, keepdims=True)


def window_start(z):
    return pl.multiple_of(128 * ((5 * z) // 4), 128)


SEMS = {
    "gr": ND, "rr": NP * NS, "ri": NS, "wy": NY, "wx": NX, "rl": NX, "na": NY, "ga": NP * NY,
    "dn": NY, "c": 5, "x": NR * NX, "z": NR * NZ, "f": 3, "g1": NS, "g2": ND,
}


def kernel(
    q_ref, k_ref, v_ref, resid_ref, llm_ref, slot_ref, mask_ref, wup_ref, wdown_ref, ngain_ref,
    gq_ref, gk_ref, gv_ref, gresid_ref, up_ref, down_ref, ggain_ref,
    rs, rr, ids, ri, gsh, gr, wu, wd, ra, la, gate, dact, dns, dnr, gt, cr, xs, xr, zs, zr,
    fs, fu, fd, gp, gs1, gp2, gs2, probs, att, unit, inv, s_loc, *sems,
):
    names = list(SEMS)
    send = {n: sems[2 * i] for i, n in enumerate(names)}
    recv = {n: sems[2 * i + 1] for i, n in enumerate(names)}
    s = lax.axis_index("seq")
    d = lax.axis_index("dp")
    z, c = s // 2, s % 2
    y, x = d // NX, d % NX
    scale = 1.0 / math.sqrt(HDIM)

    def remote(src, dst, name, at, to_s, to_d, at_recv=None):
        return pltpu.make_async_remote_copy(
            src_ref=src,
            dst_ref=dst,
            send_sem=send[name].at[at],
            recv_sem=recv[name].at[at if at_recv is None else at_recv],
            device_id=(to_s, to_d),
            device_id_type=MESH,
        )

    def y_peer(k):
        return ((y + k) % NY) * NX + x

    def x_peer(k):
        return y * NX + (x + k) % NX

    barrier = pltpu.get_barrier_semaphore()
    for k in range(1, NS):
        pl.semaphore_signal(barrier, inc=1, device_id=((s + k) % NS, d), device_id_type=MESH)
    for k in range(1, ND):
        pl.semaphore_signal(barrier, inc=1, device_id=(s, (d + k) % ND), device_id_type=MESH)
    from_s = 2 * (d // 2) + 1
    own_final = jnp.logical_and(from_s == s, s == d)

    @pl.when(jnp.logical_not(own_final))
    def _():
        pl.semaphore_signal(barrier, inc=1, device_id=(from_s, s), device_id_type=MESH)

    slot_row = slot_ref[...].astype(F32)
    slot_col = to_column(slot_row)
    owner_row = jnp.floor(slot_row * (1.0 / TOK))
    owner_col = jnp.floor(slot_col * (1.0 / TOK))
    at0, at1 = iota((POS, POS), 0), iota((POS, POS), 1)
    same = owner_col == owner_row
    rank_row = jnp.sum(jnp.where(same & (at0 < at1), 1.0, 0.0), axis=0, keepdims=True)
    rank_col = jnp.sum(jnp.where(same & (at1 < at0), 1.0, 0.0), axis=1, keepdims=True)
    target_row = jnp.where(slot_row >= 0.0, owner_row * CAP + rank_row, -1.0)
    target_col = jnp.where(slot_col >= 0.0, owner_col * CAP + rank_col, -1.0)
    hit = iota((NS * CAP, POS), 0).astype(F32) == target_row
    pick = jnp.where(hit, 1.0, 0.0).astype(BF)
    for p in range(NP):
        rs[p] = mm(pick, llm_ref[:, PW * p : PW * p + PW], 1, 0).astype(BF).reshape(NS, CAP, PW)
    lane = iota((1, 128), 1)
    lane_slot = (lane % CAP).astype(F32)
    mine = lane // CAP == s % 4
    landing = slot_col - owner_col * TOK + 1.0
    for o in range(NS):
        found = jnp.where((target_col == lane_slot + float(o * CAP)) & mine, landing, 0.0)
        ids[o] = jnp.sum(found, axis=0, keepdims=True) - 1.0
    ngain_col = to_column(ngain_ref[...].astype(F32))
    place_gain = iota((ROWS_DP, D), 1) == iota((ROWS_DP, D), 0) + d * ROWS_DP
    gsh[...] = jnp.sum(jnp.where(place_gain, ngain_col, 0.0), axis=0, keepdims=True)

    pl.semaphore_wait(barrier, NS + ND - 2 + 2 * c - jnp.where(own_final, 1, 0))

    def gain_copy(k):
        return remote(gsh, gr.at[d], "gr", k, s, (d + k) % ND)

    def row_copy(p, k):
        to = (s + k) % NS
        return remote(rs.at[p, to], rr.at[p, s], "rr", p * NS + k, to, d)

    def id_copy(k):
        to = (s + k) % NS
        return remote(ids.at[to], ri.at[s], "ri", k, to, d)

    far_first = (8, 7, 9, 6, 10, 5, 11, 4, 12, 3, 13, 2, 14, 1, 15)
    for k in far_first:
        id_copy(k).start()
    for k in far_first:
        row_copy(0, k).start()
    for k in range(1, ND):
        gain_copy(k).start()

    def quarter(q):
        return wup_ref.at[:, pl.ds(pl.multiple_of(q * FQ, 128), FQ)]

    def wy_copy(k):
        return remote(quarter((y + k) % NY), wu.at[y, x], "wy", k, s, y_peer(k))

    def ux_copy(k):
        return remote(wu.at[:, x], wu.at[:, x], "wx", k, s, x_peer(k))

    def dx_copy(k):
        return remote(wd.at[x], wd.at[x], "wx", k, s, x_peer(k))

    def ul_copy(k):
        at = (x + NX - k) % NX
        return remote(wu.at[:, at], wu.at[:, at], "rl", k, s + 1, d)

    def dl_copy(k):
        at = (x + NX - k) % NX
        return remote(wd.at[at], wd.at[at], "rl", k, s - 1, d)

    own_up = pltpu.make_async_copy(quarter(y), wu.at[y, x], s_loc.at[0])
    own_down = pltpu.make_async_copy(wdown_ref, wd.at[x], s_loc.at[1])

    @pl.when(c == 0)
    def _():
        for k in (2, 1, 3):
            wy_copy(k).start()
        own_up.start()
        own_up.wait()

    @pl.when(c == 1)
    def _():
        own_down.start()
        own_down.wait()
        for k in (2, 1, 3):
            dx_copy(k).start()
        dl_copy(0).start()

    for p in range(1, NP):
        for k in far_first:
            row_copy(p, k).start()
    for p in range(NP):
        rr[p, s] = rs[p, s]
    ri[s] = ids[s]

    row_late = iota((TOK, TOK), 0) >= BLK
    col_late = iota((TOK, TOK), 1) >= BLK
    flags = [[mask_ref[0, i : i + 1, j : j + 1] for j in range(2)] for i in range(2)]
    allowed = (
        jnp.where(
            row_late,
            jnp.where(col_late, flags[1][1], flags[1][0]),
            jnp.where(col_late, flags[0][1], flags[0][0]),
        )
        > 0
    )

    def attend(h):
        at = slice(HDIM * h, HDIM * h + HDIM)
        scores = mm(q_ref[:, at], k_ref[:, at], 1, 1) * scale
        masked = jnp.where(allowed, scores, -jnp.inf)
        highest = jnp.max(masked, axis=1, keepdims=True)
        terms = jnp.where(allowed, jnp.exp(masked - highest), 0.0)
        prob = terms * (1.0 / jnp.sum(terms, axis=1, keepdims=True))
        probs[h] = prob
        att[:, at] = mm(prob.astype(BF), v_ref[:, at], 1, 0).astype(BF)

    for h in range(HEADS // 2):
        attend(h)

    @pl.when(c == 0)
    def _():
        for k in range(1, NY):
            wy_copy(k).wait_recv()
        for k in (2, 1, 3):
            ux_copy(k).start()
        ul_copy(0).start()

    for h in range(HEADS // 2, HEADS):
        attend(h)

    gr[d] = gsh[...]
    for k in range(1, ND):
        gain_copy(k).wait_recv()
    gain_full = jnp.sum(gr[...], axis=0)

    def unit_step(i, carry):
        rows = pl.ds(pl.multiple_of(i * 32, 32), 32)
        hidden = resid_ref[rows, :].astype(F32) + att[rows, :].astype(F32)
        center = jnp.mean(hidden, axis=1, keepdims=True)
        away = hidden - center
        inverse = lax.rsqrt(jnp.mean(away * away, axis=1, keepdims=True) + 1e-06)
        inv[rows, :] = inverse
        out = away * inverse
        unit[rows, :] = out
        ra[0, y, rows, :] = (out * gain_full).astype(BF)
        return carry

    lax.fori_loop(0, TOK // 32, unit_step, 0)

    def na_copy(k):
        return remote(ra.at[0, y], ra.at[0, y], "na", k, s, y_peer(k))

    for k in (2, 1, 3):
        na_copy(k).start()

    @pl.when(c == 1)
    def _():
        for k in (1, 3, 2):
            dx_copy(k).wait_recv()
            dl_copy(k).start()

    for k in range(1, NS):
        id_copy(k).wait_recv()
    token = iota((TOK, 128), 0).astype(F32)
    place = jnp.concatenate(
        [
            jnp.where(token == jnp.max(ri[4 * j : 4 * j + 4], axis=0), 1.0, 0.0).astype(BF)
            for j in range(4)
        ],
        axis=1,
    )

    def piece(p):
        return slice(PW * p, PW * p + PW)

    def ga_copy(p, k):
        view = ra.at[1, y, :, piece(p)]
        return remote(view, view, "ga", p * NY + k, s, y_peer(k))

    def rows_in(p):
        for k in range(1, NS):
            row_copy(p, k).wait_recv()
        ra[1, y, :, piece(p)] = mm(place, rr[p].reshape(NS * CAP, PW), 1, 0).astype(BF)
        for k in (2, 1, 3):
            ga_copy(p, k).start()

    rows_in(0)
    rows_in(1)
    rows_in(2)

    @pl.when(c == 0)
    def _():
        for k in (1, 3, 2):
            ux_copy(k).wait_recv()
            ul_copy(k).start()

    @pl.when(c == 1)
    def _():
        for k in range(NX):
            ul_copy(k).wait_recv()

    for k in range(1, NY):
        na_copy(k).wait_recv()
    half = 2 * TOK

    def up_step(i, carry):
        rows = pl.ds(pl.multiple_of(i * half, half), half)
        pre = mm(ra[0, pl.ds(2 * i, 2)].reshape(half, D), wu[...].reshape(D, FQ), 1, 0)
        sig = jax.nn.sigmoid(1.702 * pre)
        la[1, rows, :] = (pre * sig).astype(BF)
        gate[rows, :] = sig + 1.702 * pre * sig * (1.0 - sig)
        return carry

    lax.fori_loop(0, 2, up_step, 0)

    rows_in(3)
    rows_in(4)

    @pl.when(c == 0)
    def _():
        for k in range(NX):
            dl_copy(k).wait_recv()

    def cd_copy(p):
        return remote(gt.at[1, :, piece(p)], cr.at[:, piece(p)], "c", p, s + 1, d)

    def cu_copy(i):
        rows = slice(128 * i, 128 * i + 128)
        return remote(gt.at[0, rows], cr.at[rows], "c", i, s - 1, d)

    def down_in(p):
        cd_copy(p).wait_recv()
        xs[:, piece(p)] = (
            gt[1, :, piece(p)].astype(F32) + cr[:, piece(p)].astype(F32)
        ).astype(BF)

    for p in range(NP):
        for k in range(1, NY):
            ga_copy(p, k).wait_recv()
        grads = ra[1, :, :, piece(p)].reshape(NY * TOK, PW)
        part = mm(grads, wd[:, :, piece(p)].reshape(FQ, PW), 1, 1)
        dact[...] = part if p == 0 else dact[...] + part
        gt[1, :, piece(p)] = mm(la[1], grads, 0, 0).astype(BF)

        @pl.when(c == 0)
        def _(p=p):
            cd_copy(p).start()

        if p > 0:

            @pl.when(c == 1)
            def _(p=p):
                down_in(p - 1)

    la[0] = (dact[...] * gate[...]).astype(BF)

    def x_copy(r, k):
        to = (x + k) % NX
        rows = pl.ds(pl.multiple_of(to * FF_DP + r * RW, RW), RW)
        return remote(
            xs.at[rows], xr.at[x, pl.ds(r * RW, RW)], "x", r * NX + k, s, y * NX + to
        )

    @pl.when(c == 1)
    def _():
        down_in(NP - 1)
        for r in range(NR):
            for k in (2, 1, 3):
                x_copy(r, k).start()

    for i in range(FQ // 128):
        rows = slice(128 * i, 128 * i + 128)
        gt[0, rows, :] = mm(la[0, :, rows], ra[0].reshape(NY * TOK, D), 0, 0).astype(BF)

        @pl.when(c == 1)
        def _(i=i):
            cu_copy(i).start()

    def norm_step(i, acc):
        rows = pl.ds(pl.multiple_of(i * half, half), half)
        part = mm(la[0, rows, :], wu[...].reshape(D, FQ), 1, 1)
        dns[pl.ds(2 * i, 2)] = part.astype(BF).reshape(2, TOK, D)
        normed = ra[0, pl.ds(2 * i, 2)].reshape(half, D).astype(F32)
        return acc + jnp.sum(part * normed, axis=0, keepdims=True)

    gp[...] = lax.fori_loop(0, 2, norm_step, jnp.zeros((1, D), F32))

    def dn_copy(k):
        to = (y + k) % NY
        return remote(dns.at[to], dnr.at[y], "dn", k, s, to * NX + x)

    for k in (2, 1, 3):
        dn_copy(k).start()

    def g1_copy(k):
        return remote(gp, gs1.at[s], "g1", k, (s + k) % NS, d)

    for k in range(1, NS):
        g1_copy(k).start()

    @pl.when(c == 0)
    def _():
        for i in range(FQ // 128):
            cu_copy(i).wait_recv()
        for r in range(NR):
            for b in range(NX):
                rows = pl.ds(b * FF_DP + r * RW, RW)
                xs[rows, :] = (gt[0, rows, :].astype(F32) + cr[rows, :].astype(F32)).astype(BF)
            for k in (2, 1, 3):
                x_copy(r, k).start()

    def z_copy(r, k):
        to = (z + k) % NZ
        rows = pl.ds(r * RW, RW)
        return remote(
            zs.at[rows, pl.ds(window_start(to), WIN)],
            zr.at[z, rows],
            "z",
            r * NZ + k,
            2 * to + c,
            d,
        )

    for r in range(NR):
        rows = pl.ds(r * RW, RW)
        own = pl.ds(pl.multiple_of(x * FF_DP + r * RW, RW), RW)
        for k in range(1, NX):
            x_copy(r, k).wait_recv()
        xr[x, rows] = xs[own, :]
        zs[rows, :] = jnp.sum(xr[:, rows, :].astype(F32), axis=0).astype(BF)
        for k in (4, 3, 5, 2, 6, 1, 7):
            z_copy(r, k).start()
        zr[z, rows] = zs[rows, pl.ds(window_start(z), WIN)]

    gs1[s] = gp[...]
    for k in range(1, NS):
        g1_copy(k).wait_recv()
    gp2[...] = jnp.sum(gs1[...], axis=0)

    def g2_copy(k):
        return remote(gp2, gs2.at[d], "g2", k, s, (d + k) % ND)

    for k in range(1, ND):
        g2_copy(k).start()

    dnr[y] = dns[y]
    for k in range(1, NY):
        dn_copy(k).wait_recv()
    gain_again = jnp.sum(gr[...], axis=0)

    def resid_step(i, carry):
        rows = pl.ds(pl.multiple_of(i * 32, 32), 32)
        d_unit = jnp.sum(dnr[:, rows, :].astype(F32), axis=0) * gain_again
        normal = unit[rows, :]
        first = jnp.mean(d_unit, axis=1, keepdims=True)
        second = jnp.mean(d_unit * normal, axis=1, keepdims=True)
        d_hidden = inv[rows, :] * (d_unit - first - normal * second)
        gresid_ref[rows, :] = (ra[1, y, rows, :].astype(F32) + d_hidden).astype(BF)
        return carry

    lax.fori_loop(0, TOK // 32, resid_step, 0)

    for h in range(HEADS):
        at = slice(HDIM * h, HDIM * h + HDIM)
        grad = gresid_ref[:, at]
        prob = probs[h]
        gv_ref[:, at] = mm(prob.astype(BF), grad, 0, 0).astype(BF)
        d_probs = mm(grad, v_ref[:, at], 1, 1)
        delta = jnp.sum(
            grad.astype(F32) * att[:, at].astype(F32), axis=1, keepdims=True
        )
        d_scores = (prob * (d_probs - delta) * scale).astype(BF)
        gq_ref[:, at] = mm(d_scores, k_ref[:, at], 1, 0).astype(BF)
        gk_ref[:, at] = mm(d_scores, q_ref[:, at], 0, 0).astype(BF)

    factor = 1.0 / math.sqrt(NS * ND * TOK)
    gs2[d] = gp2[...]
    for k in range(1, ND):
        g2_copy(k).wait_recv()
    ggain_ref[...] = jnp.sum(gs2[...], axis=0) * factor / gain_again

    for r in range(NR):
        for k in range(1, NZ):
            z_copy(r, k).wait_recv()
    fs[...] = (jnp.sum(zr[...].astype(F32), axis=0) * factor).astype(BF)

    u_copy = remote(fs, fu, "f", 0, s + 1, d)
    d0_copy = remote(fs, fd, "f", 1, d, 2 * z)
    d1_copy = remote(fs, fd, "f", 2, d, 2 * z + 1, 1)
    own_down_out = pltpu.make_async_copy(fs, fd, s_loc.at[2])

    def chosen(first):
        return jnp.where(
            iota((ROWS_DP, WIN), 1) == iota((ROWS_DP, WIN), 0) + first, 1.0, 0.0
        ).astype(BF)

    own_lanes = chosen(32 * (z % 4) + ROWS_DP * c)

    @pl.when(c == 0)
    def _():
        u_copy.start()
        up_ref[...] = mm(own_lanes, fs[...], 1, 1).astype(BF)

    @pl.when(c == 1)
    def _():
        d0_copy.start()

        @pl.when(s == d)
        def _():
            own_down_out.start()
            own_down_out.wait()

        @pl.when(s != d)
        def _():
            d1_copy.start()

        u_copy.wait_recv()
        up_ref[...] = mm(own_lanes, fu[...], 1, 1).astype(BF)

    @pl.when(jnp.logical_not(own_final))
    def _():
        d0_copy.wait_recv()

    down_ref[...] = mm(
        fd[...], chosen(32 * ((d // 2) % 4) + ROWS_DP * (d % 2)), 1, 1
    ).astype(BF)

    @pl.when(c == 0)
    def _():
        u_copy.wait_send()
        for k in range(1, NY):
            wy_copy(k).wait_send()
        for k in range(1, NX):
            ux_copy(k).wait_send()
        for k in range(NX):
            ul_copy(k).wait_send()
        for p in range(NP):
            cd_copy(p).wait_send()

    @pl.when(c == 1)
    def _():
        d0_copy.wait_send()

        @pl.when(s != d)
        def _():
            d1_copy.wait_send()

        for k in range(1, NX):
            dx_copy(k).wait_send()
        for k in range(NX):
            dl_copy(k).wait_send()
        for i in range(FQ // 128):
            cu_copy(i).wait_send()

    for k in range(1, NS):
        for p in range(NP):
            row_copy(p, k).wait_send()
        id_copy(k).wait_send()
        g1_copy(k).wait_send()
    for k in range(1, ND):
        gain_copy(k).wait_send()
        g2_copy(k).wait_send()
    for k in range(1, NY):
        na_copy(k).wait_send()
        for p in range(NP):
            ga_copy(p, k).wait_send()
        dn_copy(k).wait_send()
    for r in range(NR):
        for k in range(1, NX):
            x_copy(r, k).wait_send()
        for k in range(1, NZ):
            z_copy(r, k).wait_send()


def layer(*args):
    vm = pl.BlockSpec(memory_space=pltpu.VMEM)
    hbm = pl.BlockSpec(memory_space=pl.ANY)
    sem = pltpu.SemaphoreType.DMA
    sems = [sem((4,))]
    for n in SEMS.values():
        sems += [sem((n,)), sem((n,))]
    out = jax.ShapeDtypeStruct
    return pl.pallas_call(
        kernel,
        out_shape=(
            out((TOK, D), BF),
            out((TOK, D), BF),
            out((TOK, D), BF),
            out((TOK, D), BF),
            out((ROWS_DP, FF_DP), BF),
            out((FF_DP, ROWS_DP), BF),
            out((1, D), F32),
        ),
        in_specs=[vm] * 7 + [hbm, hbm, vm],
        out_specs=(vm,) * 7,
        scratch_shapes=[
            pltpu.VMEM((NP, NS, CAP, PW), BF),
            pltpu.VMEM((NP, NS, CAP, PW), BF),
            pltpu.VMEM((NS, 1, 128), F32),
            pltpu.VMEM((NS, 1, 128), F32),
            pltpu.VMEM((1, D), F32),
            pltpu.VMEM((ND, 1, D), F32),
            pltpu.VMEM((NY, NX, ROWS_DP, FQ), BF),
            pltpu.VMEM((NX, FF_DP, D), BF),
            pltpu.VMEM((2, NY, TOK, D), BF),
            pltpu.VMEM((2, NY * TOK, FQ), BF),
            pltpu.VMEM((NY * TOK, FQ), F32),
            pltpu.VMEM((NY * TOK, FQ), F32),
            pltpu.VMEM((NY, TOK, D), BF),
            pltpu.VMEM((NY, TOK, D), BF),
            pltpu.VMEM((2, FQ, D), BF),
            pltpu.VMEM((FQ, D), BF),
            pltpu.VMEM((FQ, D), BF),
            pltpu.VMEM((NX, FF_DP, D), BF),
            pltpu.VMEM((FF_DP, D), BF),
            pltpu.VMEM((NZ, FF_DP, WIN), BF),
            pltpu.VMEM((FF_DP, WIN), BF),
            pltpu.VMEM((FF_DP, WIN), BF),
            pltpu.VMEM((FF_DP, WIN), BF),
            pltpu.VMEM((1, D), F32),
            pltpu.VMEM((NS, 1, D), F32),
            pltpu.VMEM((1, D), F32),
            pltpu.VMEM((ND, 1, D), F32),
            pltpu.VMEM((HEADS, TOK, TOK), F32),
            pltpu.VMEM((TOK, D), BF),
            pltpu.VMEM((TOK, D), F32),
            pltpu.VMEM((TOK, 1), F32),
            *sems,
        ],
        compiler_params=pltpu.CompilerParams(
            collective_id=0, has_side_effects=True, vmem_limit_bytes=56 * 2**20
        ),
    )(*args)


def per_device(
    queries, key_rows, value_rows, resid_in, llm_grad, vision_slot, window_mask, w_up, w_down,
    norm_gain,
):
    grad_query, grad_key, grad_value, grad_resid, grad_up, grad_down, grad_gain = layer(
        queries[0],
        key_rows[0],
        value_rows[0],
        resid_in[0],
        llm_grad[0],
        vision_slot,
        window_mask,
        w_up,
        w_down,
        norm_gain.reshape(1, ROWS_DP),
    )
    return (
        grad_query[None],
        grad_key[None],
        grad_value[None],
        grad_resid[None],
        grad_up,
        grad_down,
        grad_gain.reshape(D),
    )


def solution(mesh):
    row3 = P("dp", "seq", None)
    in_specs = (
        row3,
        row3,
        row3,
        row3,
        row3,
        P("dp", "seq"),
        row3,
        P("dp", None),
        P("dp", None),
        P("dp"),
    )
    out_specs = (row3, row3, row3, row3, P("seq", "dp"), P("seq", "dp"), P())
    return jax.shard_map(
        per_device, mesh=mesh, in_specs=in_specs, out_specs=out_specs, check_vma=False
    )
```

time: 145 us -> 104 us (0.72)
  the two profiles are of different devices: /device:TPU:32 before, /device:TPU:31 now
where the time goes in v2:
time: 104 us
  Pallas kernels  95.6 us (92%)
  local copies, waits for them, and re-layouts  6.82 us (7%)
    pallas_call x1, Pallas kernels, layer(): pl.pallas_call(kernel, out_shape=(out((TOK, D), BF), out((TOK, D), BF), o...  95.6 us
    unnamed x18, local copies, waits for them, and re-layouts  6.82 us

profile of v2, /device:TPU:31, one launch (start us, length us, event | category | flops | bytes accessed | tf_op | source)
XLA Modules:
  0.0 103.7 jit_solution(9034588367532628379)
XLA Ops:
  0.6 95.6 %shard_map.153 = (bf16[128,1280]{1,0:T(8,128)(2,1)}, bf16[128,1280]{1,0:T(8,128)(2,1)}, bf16[128,1280]{1,0:T(8,128)(2,1)}, bf16[128,1280]{1,0:T(8,128)(2,1)}, bf...) custom-call(bf16[128,1280]{1,0:T(8,128)(2,1)} %bitcast.11, bf16[128,1280]{1,0:T(8,128)(2,1)} %bitcast.12, ...), custom_call_target="tpu_custom_call" | custom-call | tf_op jit(solution)/shard_map/pallas_call | solution.py:582
  96.2 0.0 copy-start.5
  96.2 0.7 copy-done.5
  96.9 0.6 reduce
  97.5 0.0 copy-start.2
  97.5 1.8 %copy.23 = bf16[1,128,1280]{2,1,0:T(8,128)(2,1)} copy(bf16[1,128,1280]{2,1,0:T(8,128)(2,1)} %bitcast.18) | data formatting | bytes 655360
  99.3 0.0 copy-done.2
  99.3 0.0 copy-start.1
  99.3 0.7 copy.24
  100.0 0.4 copy-done.1
  100.4 0.0 copy-start
  100.4 0.7 copy.25
  101.1 0.4 copy-done
  101.5 0.0 copy-start.4
  101.5 0.7 copy.26
  102.2 0.1 copy-done.4
  102.2 0.0 copy-start.3
  102.2 0.6 copy.27
  102.9 0.2 copy-done.3
  103.0 0.6 copy.28
Async XLA Ops:
  96.2 0.7 copy-start.5
  97.5 1.8 %copy-start.2 = (bf16[128,1280]{1,0:T(8,128)(2,1)S(1)}, bf16[128,1280]{1,0:T(8,128)(2,1)}, u32[]{:S(2)}) copy-start(bf16[128,1280]{1,0:T(8,128)(2,1)} %get-tuple-element.15) | copy-start | bytes 983044
  99.3 1.1 %copy-start.1 = (bf16[128,1280]{1,0:T(8,128)(2,1)S(1)}, bf16[128,1280]{1,0:T(8,128)(2,1)}, u32[]{:S(2)}) copy-start(bf16[128,1280]{1,0:T(8,128)(2,1)} %get-tuple-element.16) | copy-start | bytes 983044
  100.4 1.1 %copy-start = (bf16[128,1280]{1,0:T(8,128)(2,1)S(1)}, bf16[128,1280]{1,0:T(8,128)(2,1)}, u32[]{:S(2)}) copy-start(bf16[128,1280]{1,0:T(8,128)(2,1)} %get-tuple-element.17) | copy-start | bytes 983044
  101.5 0.8 copy-start.4
  102.2 0.8 copy-start.3

commit v3 on v2

--- a/solution.py
+++ b/solution.py
@@ -52,14 +52,15 @@
 
 
 SEMS = {
-    "gr": ND, "rr": NP * NS, "ri": NS, "wy": NY, "wx": NX, "rl": NX, "na": NY, "ga": NP * NY,
+    "gr": ND, "rr": NP * NS, "ri": NS, "wy": NY, "wx": NX, "rl": NX, "na": NY, "nf": 2, "ga": NP * NY, "gf": NP * 2,
     "dn": NY, "c": 5, "x": NR * NX, "z": NR * NZ, "f": 3, "g1": NS, "g2": ND,
 }
 
 
 def kernel(
-    q_ref, k_ref, v_ref, resid_ref, llm_ref, slot_ref, mask_ref, wup_ref, wdown_ref, ngain_ref,
-    gq_ref, gk_ref, gv_ref, gresid_ref, up_ref, down_ref, ggain_ref,
+    q_hbm, k_hbm, v_hbm, resid_hbm, llm_hbm, slot_ref, mask_ref, wup_ref, wdown_ref, ngain_ref,
+    gq_hbm, gk_hbm, gv_hbm, gresid_hbm, up_ref, down_ref, ggain_ref,
+    q_ref, k_ref, v_ref, resid_ref, llm_ref, gq_ref, gk_ref, gv_ref, gresid_ref,
     rs, rr, ids, ri, gsh, gr, wu, wd, ra, la, gate, dact, dns, dnr, gt, cr, xs, xr, zs, zr,
     fs, fu, fd, gp, gs1, gp2, gs2, probs, att, unit, inv, s_loc, *sems,
 ):
@@ -87,6 +88,25 @@
 
     def x_peer(k):
         return y * NX + (x + k) % NX
+
+    def local(src, dst, at):
+        return pltpu.make_async_copy(src, dst, s_loc.at[at])
+
+    loads = [
+        local(llm_hbm, llm_ref, 3),
+        local(q_hbm, q_ref, 4),
+        local(k_hbm, k_ref, 5),
+        local(v_hbm, v_ref, 6),
+        local(resid_hbm, resid_ref, 7),
+    ]
+    stores = [
+        local(gresid_ref, gresid_hbm, 8),
+        local(gq_ref, gq_hbm, 9),
+        local(gk_ref, gk_hbm, 10),
+        local(gv_ref, gv_hbm, 11),
+    ]
+    for copy in loads:
+        copy.start()
 
     barrier = pltpu.get_barrier_semaphore()
     for k in range(1, NS):
@@ -112,6 +132,7 @@
     target_col = jnp.where(slot_col >= 0.0, owner_col * CAP + rank_col, -1.0)
     hit = iota((NS * CAP, POS), 0).astype(F32) == target_row
     pick = jnp.where(hit, 1.0, 0.0).astype(BF)
+    loads[0].wait()
     for p in range(NP):
         rs[p] = mm(pick, llm_ref[:, PW * p : PW * p + PW], 1, 0).astype(BF).reshape(NS, CAP, PW)
     lane = iota((1, 128), 1)
@@ -203,16 +224,41 @@
         > 0
     )
 
+    def window(h):
+        first, last = HDIM * h // 128, (HDIM * h + HDIM - 1) // 128
+        lanes = slice(128 * first, 128 * last + 128)
+        feature = iota((1, lanes.stop - lanes.start), 1) + lanes.start
+        inside = (feature >= HDIM * h) & (feature < HDIM * h + HDIM)
+        return lanes, jnp.where(inside, 1.0, 0.0).astype(BF)
+
+    class Tiles:
+        def __init__(self, out):
+            self.out, self.open = out, {}
+
+        def add(self, h, value):
+            first = HDIM * h // 128
+            for i in range(value.shape[1] // 128):
+                part = value[:, 128 * i : 128 * i + 128]
+                held = self.open.get(first + i)
+                self.open[first + i] = part if held is None else held + part
+            upto = HDIM * (h + 1) // 128 if h + 1 < HEADS else D // 128
+            for t in [t for t in self.open if t < upto]:
+                self.out[:, 128 * t : 128 * t + 128] = self.open.pop(t).astype(BF)
+
+    att_tiles = Tiles(att)
+
     def attend(h):
-        at = slice(HDIM * h, HDIM * h + HDIM)
-        scores = mm(q_ref[:, at], k_ref[:, at], 1, 1) * scale
+        lanes, inside = window(h)
+        scores = mm(q_ref[:, lanes], k_ref[:, lanes] * inside, 1, 1) * scale
         masked = jnp.where(allowed, scores, -jnp.inf)
         highest = jnp.max(masked, axis=1, keepdims=True)
         terms = jnp.where(allowed, jnp.exp(masked - highest), 0.0)
         prob = terms * (1.0 / jnp.sum(terms, axis=1, keepdims=True))
         probs[h] = prob
-        att[:, at] = mm(prob.astype(BF), v_ref[:, at], 1, 0).astype(BF)
-
+        att_tiles.add(h, mm(prob.astype(BF), v_ref[:, lanes] * inside, 1, 0))
+
+    for copy in loads[1:]:
+        copy.wait()
     for h in range(HEADS // 2):
         attend(h)
 
@@ -249,8 +295,18 @@
     def na_copy(k):
         return remote(ra.at[0, y], ra.at[0, y], "na", k, s, y_peer(k))
 
-    for k in (2, 1, 3):
+    for k in (1, 3):
         na_copy(k).start()
+
+    def nf_copy(way):
+        at = (y + NY - 1) % NY if way == 0 else (y + 1) % NY
+        view = ra.at[0, at, pl.ds(way * BLK, BLK)]
+        return remote(view, view, "nf", way, s, y_peer(1 if way == 0 else 3))
+
+    def n_forward():
+        for way, k in ((0, 1), (1, 3)):
+            na_copy(k).wait_recv()
+            nf_copy(way).start()
 
     @pl.when(c == 1)
     def _():
@@ -276,15 +332,25 @@
         view = ra.at[1, y, :, piece(p)]
         return remote(view, view, "ga", p * NY + k, s, y_peer(k))
 
+    def gf_copy(p, way):
+        at = (y + NY - 1) % NY if way == 0 else (y + 1) % NY
+        view = ra.at[1, at, pl.ds(way * BLK, BLK), piece(p)]
+        return remote(view, view, "gf", p * 2 + way, s, y_peer(1 if way == 0 else 3))
+
     def rows_in(p):
         for k in range(1, NS):
             row_copy(p, k).wait_recv()
         ra[1, y, :, piece(p)] = mm(place, rr[p].reshape(NS * CAP, PW), 1, 0).astype(BF)
-        for k in (2, 1, 3):
+        for k in (1, 3) if p < NP - 1 else (2, 1, 3):
             ga_copy(p, k).start()
+        if p > 0:
+            for way, k in ((0, 1), (1, 3)):
+                ga_copy(p - 1, k).wait_recv()
+                gf_copy(p - 1, way).start()
 
     rows_in(0)
     rows_in(1)
+    n_forward()
     rows_in(2)
 
     @pl.when(c == 0)
@@ -298,8 +364,8 @@
         for k in range(NX):
             ul_copy(k).wait_recv()
 
-    for k in range(1, NY):
-        na_copy(k).wait_recv()
+    for way in range(2):
+        nf_copy(way).wait_recv()
     half = 2 * TOK
 
     def up_step(i, carry):
@@ -333,9 +399,20 @@
             gt[1, :, piece(p)].astype(F32) + cr[:, piece(p)].astype(F32)
         ).astype(BF)
 
+    for k in range(1, NS):
+        for p in range(NP):
+            row_copy(p, k).wait_send()
+        id_copy(k).wait_send()
+    for k in range(1, ND):
+        gain_copy(k).wait_send()
+
     for p in range(NP):
-        for k in range(1, NY):
-            ga_copy(p, k).wait_recv()
+        if p < NP - 1:
+            for way in range(2):
+                gf_copy(p, way).wait_recv()
+        else:
+            for k in range(1, NY):
+                ga_copy(p, k).wait_recv()
         grads = ra[1, :, :, piece(p)].reshape(NY * TOK, PW)
         part = mm(grads, wd[:, :, piece(p)].reshape(FQ, PW), 1, 1)
         dact[...] = part if p == 0 else dact[...] + part
@@ -367,14 +444,6 @@
             for k in (2, 1, 3):
                 x_copy(r, k).start()
 
-    for i in range(FQ // 128):
-        rows = slice(128 * i, 128 * i + 128)
-        gt[0, rows, :] = mm(la[0, :, rows], ra[0].reshape(NY * TOK, D), 0, 0).astype(BF)
-
-        @pl.when(c == 1)
-        def _(i=i):
-            cu_copy(i).start()
-
     def norm_step(i, acc):
         rows = pl.ds(pl.multiple_of(i * half, half), half)
         part = mm(la[0, rows, :], wu[...].reshape(D, FQ), 1, 1)
@@ -396,6 +465,14 @@
 
     for k in range(1, NS):
         g1_copy(k).start()
+
+    for i in range(FQ // 128):
+        rows = slice(128 * i, 128 * i + 128)
+        gt[0, rows, :] = mm(la[0, :, rows], ra[0].reshape(NY * TOK, D), 0, 0).astype(BF)
+
+        @pl.when(c == 1)
+        def _(i=i):
+            cu_copy(i).start()
 
     @pl.when(c == 0)
     def _():
@@ -459,18 +536,22 @@
 
     lax.fori_loop(0, TOK // 32, resid_step, 0)
 
+    stores[0].start()
+    gq_tiles, gk_tiles, gv_tiles = Tiles(gq_ref), Tiles(gk_ref), Tiles(gv_ref)
     for h in range(HEADS):
-        at = slice(HDIM * h, HDIM * h + HDIM)
-        grad = gresid_ref[:, at]
+        lanes, inside = window(h)
+        grad = gresid_ref[:, lanes] * inside
         prob = probs[h]
-        gv_ref[:, at] = mm(prob.astype(BF), grad, 0, 0).astype(BF)
-        d_probs = mm(grad, v_ref[:, at], 1, 1)
+        gv_tiles.add(h, mm(prob.astype(BF), grad, 0, 0))
+        d_probs = mm(grad, v_ref[:, lanes], 1, 1)
         delta = jnp.sum(
-            grad.astype(F32) * att[:, at].astype(F32), axis=1, keepdims=True
+            grad.astype(F32) * att[:, lanes].astype(F32), axis=1, keepdims=True
         )
         d_scores = (prob * (d_probs - delta) * scale).astype(BF)
-        gq_ref[:, at] = mm(d_scores, k_ref[:, at], 1, 0).astype(BF)
-        gk_ref[:, at] = mm(d_scores, q_ref[:, at], 0, 0).astype(BF)
+        gq_tiles.add(h, mm(d_scores, k_ref[:, lanes] * inside, 1, 0))
+        gk_tiles.add(h, mm(d_scores, q_ref[:, lanes] * inside, 0, 0))
+    for copy in stores[1:]:
+        copy.start()
 
     factor = 1.0 / math.sqrt(NS * ND * TOK)
     gs2[d] = gp2[...]
@@ -552,18 +633,22 @@
             cu_copy(i).wait_send()
 
     for k in range(1, NS):
-        for p in range(NP):
-            row_copy(p, k).wait_send()
-        id_copy(k).wait_send()
         g1_copy(k).wait_send()
     for k in range(1, ND):
-        gain_copy(k).wait_send()
         g2_copy(k).wait_send()
     for k in range(1, NY):
-        na_copy(k).wait_send()
+        if k != 2:
+            na_copy(k).wait_send()
         for p in range(NP):
-            ga_copy(p, k).wait_send()
+            if k != 2 or p == NP - 1:
+                ga_copy(p, k).wait_send()
         dn_copy(k).wait_send()
+    for way in range(2):
+        nf_copy(way).wait_send()
+        for p in range(NP - 1):
+            gf_copy(p, way).wait_send()
+    for copy in stores:
+        copy.wait()
     for r in range(NR):
         for k in range(1, NX):
             x_copy(r, k).wait_send()
@@ -575,7 +660,7 @@
     vm = pl.BlockSpec(memory_space=pltpu.VMEM)
     hbm = pl.BlockSpec(memory_space=pl.ANY)
     sem = pltpu.SemaphoreType.DMA
-    sems = [sem((4,))]
+    sems = [sem((12,))]
     for n in SEMS.values():
         sems += [sem((n,)), sem((n,))]
     out = jax.ShapeDtypeStruct
@@ -590,9 +675,12 @@
             out((FF_DP, ROWS_DP), BF),
             out((1, D), F32),
         ),
-        in_specs=[vm] * 7 + [hbm, hbm, vm],
-        out_specs=(vm,) * 7,
+        in_specs=[hbm] * 5 + [vm, vm, hbm, hbm, vm],
+        out_specs=(hbm,) * 4 + (vm,) * 3,
         scratch_shapes=[
+            *[pltpu.VMEM((TOK, D), BF)] * 4,
+            pltpu.VMEM((POS, D), BF),
+            *[pltpu.VMEM((TOK, D), BF)] * 4,
             pltpu.VMEM((NP, NS, CAP, PW), BF),
             pltpu.VMEM((NP, NS, CAP, PW), BF),
             pltpu.VMEM((NS, 1, 128), F32),
@@ -632,11 +720,48 @@
     )(*args)
 
 
+def hand_out_kernel(*refs):
+    n = 7
+    ins, outs, held, taken, done = refs[:n], refs[n : 2 * n], refs[2 * n : -2], refs[-2], refs[-1]
+    into = [pltpu.make_async_copy(ins[i], held[i], taken.at[i]) for i in range(4)]
+    out = [
+        pltpu.make_async_copy(held[i] if i < 4 else ins[i], outs[i], done.at[i])
+        for i in range(n - 1)
+    ]
+    for copy in into:
+        copy.start()
+    for copy in out[4:]:
+        copy.start()
+    outs[n - 1][...] = ins[n - 1][0, :]
+    for i in range(4):
+        into[i].wait()
+        out[i].start()
+    for copy in out:
+        copy.wait()
+
+
+def hand_out(arrays):
+    vm = pl.BlockSpec(memory_space=pltpu.VMEM)
+    hbm = pl.BlockSpec(memory_space=pl.ANY)
+    return pl.pallas_call(
+        hand_out_kernel,
+        out_shape=tuple(jax.ShapeDtypeStruct(a.shape, a.dtype) for a in arrays[:-1])
+        + (jax.ShapeDtypeStruct((D,), F32),),
+        in_specs=[hbm] * 4 + [vm] * 3,
+        out_specs=(hbm,) * 6 + (vm,),
+        scratch_shapes=[
+            *[pltpu.VMEM((TOK, D), BF)] * 4,
+            pltpu.SemaphoreType.DMA((4,)),
+            pltpu.SemaphoreType.DMA((6,)),
+        ],
+    )(*arrays)
+
+
 def per_device(
     queries, key_rows, value_rows, resid_in, llm_grad, vision_slot, window_mask, w_up, w_down,
     norm_gain,
 ):
-    grad_query, grad_key, grad_value, grad_resid, grad_up, grad_down, grad_gain = layer(
+    results = layer(
         queries[0],
         key_rows[0],
         value_rows[0],
@@ -648,6 +773,7 @@
         w_down,
         norm_gain.reshape(1, ROWS_DP),
     )
+    grad_query, grad_key, grad_value, grad_resid, grad_up, grad_down, grad_gain = hand_out(results)
     return (
         grad_query[None],
         grad_key[None],
@@ -655,7 +781,7 @@
         grad_resid[None],
         grad_up,
         grad_down,
-        grad_gain.reshape(D),
+        grad_gain,
     )
 
 

time: 104 us -> 94.6 us (0.910)
  local copies, waits for them, and re-layouts: 6.82 us -> 0 us
  Pallas kernels: 95.6 us -> 93.5 us
    unnamed x18 -> x0, local copies, waits for them, and re-layouts: 6.82 us -> none
    pallas_call x1, Pallas kernels: 95.6 us -> 89.9 us  [layer(): pl.pallas_call(kernel, out_shape=(out((TOK, D), BF), out((TOK, D), BF), o...]
    pallas_call x0 -> x1, Pallas kernels: none -> 3.54 us  [hand_out(): pl.pallas_call(hand_out_kernel, out_shape=tuple((jax.ShapeDtypeStruct(a.s...]
where the time goes in v3:
time: 94.6 us; the launch traced here: 94.3 us
  Pallas kernels  93.5 us (99%)
    pallas_call x1, Pallas kernels, layer(): pl.pallas_call(kernel, out_shape=(out((TOK, D), BF), out((TOK, D), BF), o...  89.9 us
    pallas_call x1, Pallas kernels, hand_out(): pl.pallas_call(hand_out_kernel, out_shape=tuple((jax.ShapeDtypeStruct(a.s...  3.54 us

profile of v3, /device:TPU:31, one launch (start us, length us, event | category | flops | bytes accessed | tf_op | source)
XLA Modules:
  0.0 94.3 jit_solution(17941122463374506885)
XLA Ops:
  0.6 89.9 %shard_map.153 = (bf16[128,1280]{1,0:T(8,128)(2,1)}, bf16[128,1280]{1,0:T(8,128)(2,1)}, bf16[128,1280]{1,0:T(8,128)(2,1)}, bf16[128,1280]{1,0:T(8,128)(2,1)}, bf...) custom-call(bf16[128,1280]{1,0:T(8,128)(2,1)} %bitcast.11, bf16[128,1280]{1,0:T(8,128)(2,1)} %bitcast.12, ...), custom_call_target="tpu_custom_call" | custom-call | tf_op jit(solution)/shard_map/pallas_call | solution.py:667
  90.6 3.5 %shard_map.154 = (bf16[128,1280]{1,0:T(8,128)(2,1)}, bf16[128,1280]{1,0:T(8,128)(2,1)}, bf16[128,1280]{1,0:T(8,128)(2,1)}, bf16[128,1280]{1,0:T(8,128)(2,1)}, bf...) custom-call(bf16[128,1280]{1,0:T(8,128)(2,1)} %get-tuple-element.21.refs_0_, ...), custom_call_target="tpu_custom_call" | custom-call | tf_op jit(solution)/shard_map/pallas_call | solution.py:746

commit v4 on v3

--- a/solution.py
+++ b/solution.py
@@ -24,8 +24,10 @@
 WIN = 256
 NP = 5
 PW = D // NP
+NRELAY = 3
 NR = 5
 RW = FF_DP // NR
+WHOLE = ((0,), (1, 2), (3,), (4, 5), (6, 7))
 MESH = pl.DeviceIdType.MESH
 BF = jnp.bfloat16
 F32 = jnp.float32
@@ -341,9 +343,9 @@
         for k in range(1, NS):
             row_copy(p, k).wait_recv()
         ra[1, y, :, piece(p)] = mm(place, rr[p].reshape(NS * CAP, PW), 1, 0).astype(BF)
-        for k in (1, 3) if p < NP - 1 else (2, 1, 3):
+        for k in (1, 3) if p < NRELAY else (2, 1, 3):
             ga_copy(p, k).start()
-        if p > 0:
+        if 0 < p <= NRELAY:
             for way, k in ((0, 1), (1, 3)):
                 ga_copy(p - 1, k).wait_recv()
                 gf_copy(p - 1, way).start()
@@ -378,9 +380,6 @@
 
     lax.fori_loop(0, 2, up_step, 0)
 
-    rows_in(3)
-    rows_in(4)
-
     @pl.when(c == 0)
     def _():
         for k in range(NX):
@@ -399,15 +398,8 @@
             gt[1, :, piece(p)].astype(F32) + cr[:, piece(p)].astype(F32)
         ).astype(BF)
 
-    for k in range(1, NS):
-        for p in range(NP):
-            row_copy(p, k).wait_send()
-        id_copy(k).wait_send()
-    for k in range(1, ND):
-        gain_copy(k).wait_send()
-
-    for p in range(NP):
-        if p < NP - 1:
+    def down_step(p):
+        if p < NRELAY:
             for way in range(2):
                 gf_copy(p, way).wait_recv()
         else:
@@ -419,30 +411,78 @@
         gt[1, :, piece(p)] = mm(la[1], grads, 0, 0).astype(BF)
 
         @pl.when(c == 0)
-        def _(p=p):
+        def _():
             cd_copy(p).start()
 
-        if p > 0:
-
-            @pl.when(c == 1)
-            def _(p=p):
-                down_in(p - 1)
-
+    def block(i):
+        return pl.ds(pl.multiple_of(i * FF_DP, FF_DP), FF_DP)
+
+    def xd_copy(p, k):
+        to = (x + k) % NX
+        return remote(
+            xs.at[block(to), piece(p)], xr.at[x, :, piece(p)], "x", p * NX + k, s, x_peer(k)
+        )
+
+    def zd_copy(to, source):
+        first = 128 * ((5 * to) // 4)
+        return remote(
+            zs.at[:, first : first + WIN], zr.at[source], "z", to, 2 * to + c, d, source
+        )
+
+    def down_out(p):
+        down_in(p)
+        for k in (2, 1, 3):
+            xd_copy(p, k).start()
+
+    def down_sum(p):
+        for k in range(1, NX):
+            xd_copy(p, k).wait_recv()
+        xr[x, :, piece(p)] = xs[block(x), piece(p)]
+        zs[:, piece(p)] = jnp.sum(xr[:, :, piece(p)].astype(F32), axis=0).astype(BF)
+        for to in WHOLE[p]:
+
+            @pl.when(z != to)
+            def _(to=to):
+                zd_copy(to, z).start()
+
+            @pl.when(z == to)
+            def _(to=to):
+                first = 128 * ((5 * to) // 4)
+                zr[to] = zs[:, first : first + WIN]
+
+    def on_core_one(*steps):
+        @pl.when(c == 1)
+        def _():
+            for step, p in steps:
+                step(p)
+
+    down_step(0)
+    down_step(1)
+    rows_in(3)
+    on_core_one((down_out, 0), (down_out, 1))
+    down_step(2)
+    rows_in(4)
+    on_core_one((down_out, 2), (down_sum, 0), (down_sum, 1))
+    down_step(3)
+    on_core_one((down_out, 3),)
+
+    for k in range(1, NS):
+        for p in range(NP):
+            row_copy(p, k).wait_send()
+        id_copy(k).wait_send()
+    for k in range(1, ND):
+        gain_copy(k).wait_send()
+
+    down_step(4)
     la[0] = (dact[...] * gate[...]).astype(BF)
+    on_core_one((down_out, 4),)
 
     def x_copy(r, k):
         to = (x + k) % NX
         rows = pl.ds(pl.multiple_of(to * FF_DP + r * RW, RW), RW)
         return remote(
-            xs.at[rows], xr.at[x, pl.ds(r * RW, RW)], "x", r * NX + k, s, y * NX + to
+            xs.at[rows], xr.at[x, pl.ds(r * RW, RW)], "x", r * NX + k, s, x_peer(k)
         )
-
-    @pl.when(c == 1)
-    def _():
-        down_in(NP - 1)
-        for r in range(NR):
-            for k in (2, 1, 3):
-                x_copy(r, k).start()
 
     def norm_step(i, acc):
         rows = pl.ds(pl.multiple_of(i * half, half), half)
@@ -474,16 +514,7 @@
         def _(i=i):
             cu_copy(i).start()
 
-    @pl.when(c == 0)
-    def _():
-        for i in range(FQ // 128):
-            cu_copy(i).wait_recv()
-        for r in range(NR):
-            for b in range(NX):
-                rows = pl.ds(b * FF_DP + r * RW, RW)
-                xs[rows, :] = (gt[0, rows, :].astype(F32) + cr[rows, :].astype(F32)).astype(BF)
-            for k in (2, 1, 3):
-                x_copy(r, k).start()
+    on_core_one((down_sum, 2), (down_sum, 3), (down_sum, 4))
 
     def z_copy(r, k):
         to = (z + k) % NZ
@@ -497,16 +528,26 @@
             d,
         )
 
-    for r in range(NR):
-        rows = pl.ds(r * RW, RW)
-        own = pl.ds(pl.multiple_of(x * FF_DP + r * RW, RW), RW)
-        for k in range(1, NX):
-            x_copy(r, k).wait_recv()
-        xr[x, rows] = xs[own, :]
-        zs[rows, :] = jnp.sum(xr[:, rows, :].astype(F32), axis=0).astype(BF)
-        for k in (4, 3, 5, 2, 6, 1, 7):
-            z_copy(r, k).start()
-        zr[z, rows] = zs[rows, pl.ds(window_start(z), WIN)]
+    @pl.when(c == 0)
+    def _():
+        for i in range(FQ // 128):
+            cu_copy(i).wait_recv()
+        for r in range(NR):
+            for b in range(NX):
+                rows = pl.ds(b * FF_DP + r * RW, RW)
+                xs[rows, :] = (gt[0, rows, :].astype(F32) + cr[rows, :].astype(F32)).astype(BF)
+            for k in (2, 1, 3):
+                x_copy(r, k).start()
+        for r in range(NR):
+            rows = pl.ds(r * RW, RW)
+            own = pl.ds(pl.multiple_of(x * FF_DP + r * RW, RW), RW)
+            for k in range(1, NX):
+                x_copy(r, k).wait_recv()
+            xr[x, rows] = xs[own, :]
+            zs[rows, :] = jnp.sum(xr[:, rows, :].astype(F32), axis=0).astype(BF)
+            for k in (4, 3, 5, 2, 6, 1, 7):
+                z_copy(r, k).start()
+            zr[z, rows] = zs[rows, pl.ds(window_start(z), WIN)]
 
     gs1[s] = gp[...]
     for k in range(1, NS):
@@ -518,6 +559,36 @@
 
     for k in range(1, ND):
         g2_copy(k).start()
+
+    factor = 1.0 / math.sqrt(NS * ND * TOK)
+
+    def window_sum():
+        fs[...] = (jnp.sum(zr[...].astype(F32), axis=0) * factor).astype(BF)
+
+    u_copy = remote(fs, fu, "f", 0, s + 1, d)
+    d0_copy = remote(fs, fd, "f", 1, d, 2 * z)
+    d1_copy = remote(fs, fd, "f", 2, d, 2 * z + 1, 1)
+    own_down_out = pltpu.make_async_copy(fs, fd, s_loc.at[2])
+
+    @pl.when(c == 1)
+    def _():
+        for source in range(NZ):
+
+            @pl.when(z != source)
+            def _(source=source):
+                zd_copy(source, source).wait_recv()
+
+        window_sum()
+        d0_copy.start()
+
+        @pl.when(s == d)
+        def _():
+            own_down_out.start()
+            own_down_out.wait()
+
+        @pl.when(s != d)
+        def _():
+            d1_copy.start()
 
     dnr[y] = dns[y]
     for k in range(1, NY):
@@ -553,22 +624,11 @@
     for copy in stores[1:]:
         copy.start()
 
-    factor = 1.0 / math.sqrt(NS * ND * TOK)
     gs2[d] = gp2[...]
     for k in range(1, ND):
         g2_copy(k).wait_recv()
     ggain_ref[...] = jnp.sum(gs2[...], axis=0) * factor / gain_again
 
-    for r in range(NR):
-        for k in range(1, NZ):
-            z_copy(r, k).wait_recv()
-    fs[...] = (jnp.sum(zr[...].astype(F32), axis=0) * factor).astype(BF)
-
-    u_copy = remote(fs, fu, "f", 0, s + 1, d)
-    d0_copy = remote(fs, fd, "f", 1, d, 2 * z)
-    d1_copy = remote(fs, fd, "f", 2, d, 2 * z + 1, 1)
-    own_down_out = pltpu.make_async_copy(fs, fd, s_loc.at[2])
-
     def chosen(first):
         return jnp.where(
             iota((ROWS_DP, WIN), 1) == iota((ROWS_DP, WIN), 0) + first, 1.0, 0.0
@@ -578,22 +638,15 @@
 
     @pl.when(c == 0)
     def _():
+        for r in range(NR):
+            for k in range(1, NZ):
+                z_copy(r, k).wait_recv()
+        window_sum()
         u_copy.start()
         up_ref[...] = mm(own_lanes, fs[...], 1, 1).astype(BF)
 
     @pl.when(c == 1)
     def _():
-        d0_copy.start()
-
-        @pl.when(s == d)
-        def _():
-            own_down_out.start()
-            own_down_out.wait()
-
-        @pl.when(s != d)
-        def _():
-            d1_copy.start()
-
         u_copy.wait_recv()
         up_ref[...] = mm(own_lanes, fu[...], 1, 1).astype(BF)
 
@@ -616,6 +669,11 @@
             ul_copy(k).wait_send()
         for p in range(NP):
             cd_copy(p).wait_send()
+        for r in range(NR):
+            for k in range(1, NX):
+                x_copy(r, k).wait_send()
+            for k in range(1, NZ):
+                z_copy(r, k).wait_send()
 
     @pl.when(c == 1)
     def _():
@@ -631,6 +689,14 @@
             dl_copy(k).wait_send()
         for i in range(FQ // 128):
             cu_copy(i).wait_send()
+        for p in range(NP):
+            for k in range(1, NX):
+                xd_copy(p, k).wait_send()
+        for to in range(NZ):
+
+            @pl.when(z != to)
+            def _(to=to):
+                zd_copy(to, z).wait_send()
 
     for k in range(1, NS):
         g1_copy(k).wait_send()
@@ -640,20 +706,15 @@
         if k != 2:
             na_copy(k).wait_send()
         for p in range(NP):
-            if k != 2 or p == NP - 1:
+            if k != 2 or p >= NRELAY:
                 ga_copy(p, k).wait_send()
         dn_copy(k).wait_send()
     for way in range(2):
         nf_copy(way).wait_send()
-        for p in range(NP - 1):
+        for p in range(NRELAY):
             gf_copy(p, way).wait_send()
     for copy in stores:
         copy.wait()
-    for r in range(NR):
-        for k in range(1, NX):
-            x_copy(r, k).wait_send()
-        for k in range(1, NZ):
-            z_copy(r, k).wait_send()
 
 
 def layer(*args):

time: 94.6 us -> 95.8 us (1.013); the launches traced: 94.3 us -> 94 us
  no operation moved by 1% of the time
where the time goes in v4:
time: 95.8 us; the launch traced here: 94 us
  Pallas kernels  93.2 us (97%)
    pallas_call x1, Pallas kernels, layer(): pl.pallas_call(kernel, out_shape=(out((TOK, D), BF), out((TOK, D), BF), o...  89.7 us
    pallas_call x1, Pallas kernels, hand_out(): pl.pallas_call(hand_out_kernel, out_shape=tuple((jax.ShapeDtypeStruct(a.s...  3.54 us

profile of v4, /device:TPU:31, one launch (start us, length us, event | category | flops | bytes accessed | tf_op | source)
XLA Modules:
  0.0 94.0 jit_solution(1779816752816480938)
XLA Ops:
  0.6 89.7 %shard_map.153 = (bf16[128,1280]{1,0:T(8,128)(2,1)}, bf16[128,1280]{1,0:T(8,128)(2,1)}, bf16[128,1280]{1,0:T(8,128)(2,1)}, bf16[128,1280]{1,0:T(8,128)(2,1)}, bf...) custom-call(bf16[128,1280]{1,0:T(8,128)(2,1)} %bitcast.11, bf16[128,1280]{1,0:T(8,128)(2,1)} %bitcast.12, ...), custom_call_target="tpu_custom_call" | custom-call | tf_op jit(solution)/shard_map/pallas_call | solution.py:728
  90.3 3.5 %shard_map.154 = (bf16[128,1280]{1,0:T(8,128)(2,1)}, bf16[128,1280]{1,0:T(8,128)(2,1)}, bf16[128,1280]{1,0:T(8,128)(2,1)}, bf16[128,1280]{1,0:T(8,128)(2,1)}, bf...) custom-call(bf16[128,1280]{1,0:T(8,128)(2,1)} %get-tuple-element.21.refs_0_, ...), custom_call_target="tpu_custom_call" | custom-call | tf_op jit(solution)/shard_map/pallas_call | solution.py:807

commit v5 on v4

--- a/solution.py
+++ b/solution.py
@@ -60,8 +60,9 @@
 
 
 def kernel(
-    q_hbm, k_hbm, v_hbm, resid_hbm, llm_hbm, slot_ref, mask_ref, wup_ref, wdown_ref, ngain_ref,
-    gq_hbm, gk_hbm, gv_hbm, gresid_hbm, up_ref, down_ref, ggain_ref,
+    q_hbm, k_hbm, v_hbm, resid_hbm, llm_hbm, slot_hbm, mask_hbm, wup_ref, wdown_ref, ngain_hbm,
+    gq_hbm, gk_hbm, gv_hbm, gresid_hbm, up_hbm, down_hbm, ggain_hbm,
+    slot_ref, mask_ref, ngain_ref, up_ref, down_ref, ggain_ref,
     q_ref, k_ref, v_ref, resid_ref, llm_ref, gq_ref, gk_ref, gv_ref, gresid_ref,
     rs, rr, ids, ri, gsh, gr, wu, wd, ra, la, gate, dact, dns, dnr, gt, cr, xs, xr, zs, zr,
     fs, fu, fd, gp, gs1, gp2, gs2, probs, att, unit, inv, s_loc, *sems,
@@ -94,6 +95,13 @@
     def local(src, dst, at):
         return pltpu.make_async_copy(src, dst, s_loc.at[at])
 
+    small = [
+        local(slot_hbm, slot_ref, 12),
+        local(ngain_hbm, ngain_ref, 13),
+        local(mask_hbm, mask_ref, 14),
+    ]
+    for copy in small:
+        copy.start()
     loads = [
         local(llm_hbm, llm_ref, 3),
         local(q_hbm, q_ref, 4),
@@ -122,6 +130,8 @@
     def _():
         pl.semaphore_signal(barrier, inc=1, device_id=(from_s, s), device_id_type=MESH)
 
+    for copy in small:
+        copy.wait()
     slot_row = slot_ref[...].astype(F32)
     slot_col = to_column(slot_row)
     owner_row = jnp.floor(slot_row * (1.0 / TOK))
@@ -134,9 +144,67 @@
     target_col = jnp.where(slot_col >= 0.0, owner_col * CAP + rank_col, -1.0)
     hit = iota((NS * CAP, POS), 0).astype(F32) == target_row
     pick = jnp.where(hit, 1.0, 0.0).astype(BF)
+
+    def pack(p):
+        rs[p] = mm(pick, llm_ref[:, PW * p : PW * p + PW], 1, 0).astype(BF).reshape(NS, CAP, PW)
+
     loads[0].wait()
-    for p in range(NP):
-        rs[p] = mm(pick, llm_ref[:, PW * p : PW * p + PW], 1, 0).astype(BF).reshape(NS, CAP, PW)
+    pack(0)
+    pl.semaphore_wait(barrier, NS + ND - 2 + 2 * c - jnp.where(own_final, 1, 0))
+
+    def gain_copy(k):
+        return remote(gsh, gr.at[d], "gr", k, s, (d + k) % ND)
+
+    def row_copy(p, k):
+        to = (s + k) % NS
+        return remote(rs.at[p, to], rr.at[p, s], "rr", p * NS + k, to, d)
+
+    def id_copy(k):
+        to = (s + k) % NS
+        return remote(ids.at[to], ri.at[s], "ri", k, to, d)
+
+    far_first = (8, 7, 9, 6, 10, 5, 11, 4, 12, 3, 13, 2, 14, 1, 15)
+    for k in far_first:
+        row_copy(0, k).start()
+
+    def quarter(q):
+        return wup_ref.at[:, pl.ds(pl.multiple_of(q * FQ, 128), FQ)]
+
+    def wy_copy(k):
+        return remote(quarter((y + k) % NY), wu.at[y, x], "wy", k, s, y_peer(k))
+
+    def ux_copy(k):
+        return remote(wu.at[:, x], wu.at[:, x], "wx", k, s, x_peer(k))
+
+    def dx_copy(k):
+        return remote(wd.at[x], wd.at[x], "wx", k, s, x_peer(k))
+
+    def ul_copy(k):
+        at = (x + NX - k) % NX
+        return remote(wu.at[:, at], wu.at[:, at], "rl", k, s + 1, d)
+
+    def dl_copy(k):
+        at = (x + NX - k) % NX
+        return remote(wd.at[at], wd.at[at], "rl", k, s - 1, d)
+
+    own_up = pltpu.make_async_copy(quarter(y), wu.at[y, x], s_loc.at[0])
+    own_down = pltpu.make_async_copy(wdown_ref, wd.at[x], s_loc.at[1])
+
+    @pl.when(c == 0)
+    def _():
+        for k in (2, 1, 3):
+            wy_copy(k).start()
+        own_up.start()
+        own_up.wait()
+
+    @pl.when(c == 1)
+    def _():
+        own_down.start()
+        own_down.wait()
+        for k in (2, 1, 3):
+            dx_copy(k).start()
+        dl_copy(0).start()
+
     lane = iota((1, 128), 1)
     lane_slot = (lane % CAP).astype(F32)
     mine = lane // CAP == s % 4
@@ -148,66 +216,12 @@
     place_gain = iota((ROWS_DP, D), 1) == iota((ROWS_DP, D), 0) + d * ROWS_DP
     gsh[...] = jnp.sum(jnp.where(place_gain, ngain_col, 0.0), axis=0, keepdims=True)
 
-    pl.semaphore_wait(barrier, NS + ND - 2 + 2 * c - jnp.where(own_final, 1, 0))
-
-    def gain_copy(k):
-        return remote(gsh, gr.at[d], "gr", k, s, (d + k) % ND)
-
-    def row_copy(p, k):
-        to = (s + k) % NS
-        return remote(rs.at[p, to], rr.at[p, s], "rr", p * NS + k, to, d)
-
-    def id_copy(k):
-        to = (s + k) % NS
-        return remote(ids.at[to], ri.at[s], "ri", k, to, d)
-
-    far_first = (8, 7, 9, 6, 10, 5, 11, 4, 12, 3, 13, 2, 14, 1, 15)
     for k in far_first:
         id_copy(k).start()
-    for k in far_first:
-        row_copy(0, k).start()
     for k in range(1, ND):
         gain_copy(k).start()
-
-    def quarter(q):
-        return wup_ref.at[:, pl.ds(pl.multiple_of(q * FQ, 128), FQ)]
-
-    def wy_copy(k):
-        return remote(quarter((y + k) % NY), wu.at[y, x], "wy", k, s, y_peer(k))
-
-    def ux_copy(k):
-        return remote(wu.at[:, x], wu.at[:, x], "wx", k, s, x_peer(k))
-
-    def dx_copy(k):
-        return remote(wd.at[x], wd.at[x], "wx", k, s, x_peer(k))
-
-    def ul_copy(k):
-        at = (x + NX - k) % NX
-        return remote(wu.at[:, at], wu.at[:, at], "rl", k, s + 1, d)
-
-    def dl_copy(k):
-        at = (x + NX - k) % NX
-        return remote(wd.at[at], wd.at[at], "rl", k, s - 1, d)
-
-    own_up = pltpu.make_async_copy(quarter(y), wu.at[y, x], s_loc.at[0])
-    own_down = pltpu.make_async_copy(wdown_ref, wd.at[x], s_loc.at[1])
-
-    @pl.when(c == 0)
-    def _():
-        for k in (2, 1, 3):
-            wy_copy(k).start()
-        own_up.start()
-        own_up.wait()
-
-    @pl.when(c == 1)
-    def _():
-        own_down.start()
-        own_down.wait()
-        for k in (2, 1, 3):
-            dx_copy(k).start()
-        dl_copy(0).start()
-
     for p in range(1, NP):
+        pack(p)
         for k in far_first:
             row_copy(p, k).start()
     for p in range(NP):
@@ -462,9 +476,8 @@
     on_core_one((down_out, 0), (down_out, 1))
     down_step(2)
     rows_in(4)
-    on_core_one((down_out, 2), (down_sum, 0), (down_sum, 1))
+    on_core_one((down_out, 2),)
     down_step(3)
-    on_core_one((down_out, 3),)
 
     for k in range(1, NS):
         for p in range(NP):
@@ -475,7 +488,6 @@
 
     down_step(4)
     la[0] = (dact[...] * gate[...]).astype(BF)
-    on_core_one((down_out, 4),)
 
     def x_copy(r, k):
         to = (x + k) % NX
@@ -514,7 +526,15 @@
         def _(i=i):
             cu_copy(i).start()
 
-    on_core_one((down_sum, 2), (down_sum, 3), (down_sum, 4))
+    on_core_one(
+        (down_out, 3),
+        (down_out, 4),
+        (down_sum, 0),
+        (down_sum, 1),
+        (down_sum, 2),
+        (down_sum, 3),
+        (down_sum, 4),
+    )
 
     def z_copy(r, k):
         to = (z + k) % NZ
@@ -607,6 +627,46 @@
 
     lax.fori_loop(0, TOK // 32, resid_step, 0)
 
+    def chosen(first):
+        return jnp.where(
+            iota((ROWS_DP, WIN), 1) == iota((ROWS_DP, WIN), 0) + first, 1.0, 0.0
+        ).astype(BF)
+
+    own_lanes = chosen(32 * (z % 4) + ROWS_DP * c)
+
+    def gain_end():
+        gs2[d] = gp2[...]
+        for k in range(1, ND):
+            g2_copy(k).wait_recv()
+        ggain_ref[...] = jnp.sum(gs2[...], axis=0) * factor / gain_again
+        local(ggain_ref, ggain_hbm, 17).start()
+
+    def up_end():
+        @pl.when(c == 0)
+        def _():
+            for r in range(NR):
+                for k in range(1, NZ):
+                    z_copy(r, k).wait_recv()
+            window_sum()
+            u_copy.start()
+            up_ref[...] = mm(own_lanes, fs[...], 1, 1).astype(BF)
+
+    def outputs_end():
+        @pl.when(c == 1)
+        def _():
+            u_copy.wait_recv()
+            up_ref[...] = mm(own_lanes, fu[...], 1, 1).astype(BF)
+
+        @pl.when(jnp.logical_not(own_final))
+        def _():
+            d0_copy.wait_recv()
+
+        down_ref[...] = mm(
+            fd[...], chosen(32 * ((d // 2) % 4) + ROWS_DP * (d % 2)), 1, 1
+        ).astype(BF)
+        local(up_ref, up_hbm, 15).start()
+        local(down_ref, down_hbm, 16).start()
+
     stores[0].start()
     gq_tiles, gk_tiles, gv_tiles = Tiles(gq_ref), Tiles(gk_ref), Tiles(gv_ref)
     for h in range(HEADS):
@@ -621,42 +681,13 @@
         d_scores = (prob * (d_probs - delta) * scale).astype(BF)
         gq_tiles.add(h, mm(d_scores, k_ref[:, lanes] * inside, 1, 0))
         gk_tiles.add(h, mm(d_scores, q_ref[:, lanes] * inside, 0, 0))
+        if h == 7:
+            up_end()
+        elif h == 11:
+            outputs_end()
+            gain_end()
     for copy in stores[1:]:
         copy.start()
-
-    gs2[d] = gp2[...]
-    for k in range(1, ND):
-        g2_copy(k).wait_recv()
-    ggain_ref[...] = jnp.sum(gs2[...], axis=0) * factor / gain_again
-
-    def chosen(first):
-        return jnp.where(
-            iota((ROWS_DP, WIN), 1) == iota((ROWS_DP, WIN), 0) + first, 1.0, 0.0
-        ).astype(BF)
-
-    own_lanes = chosen(32 * (z % 4) + ROWS_DP * c)
-
-    @pl.when(c == 0)
-    def _():
-        for r in range(NR):
-            for k in range(1, NZ):
-                z_copy(r, k).wait_recv()
-        window_sum()
-        u_copy.start()
-        up_ref[...] = mm(own_lanes, fs[...], 1, 1).astype(BF)
-
-    @pl.when(c == 1)
-    def _():
-        u_copy.wait_recv()
-        up_ref[...] = mm(own_lanes, fu[...], 1, 1).astype(BF)
-
-    @pl.when(jnp.logical_not(own_final))
-    def _():
-        d0_copy.wait_recv()
-
-    down_ref[...] = mm(
-        fd[...], chosen(32 * ((d // 2) % 4) + ROWS_DP * (d % 2)), 1, 1
-    ).astype(BF)
 
     @pl.when(c == 0)
     def _():
@@ -715,13 +746,15 @@
             gf_copy(p, way).wait_send()
     for copy in stores:
         copy.wait()
+    local(up_ref, up_hbm, 15).wait()
+    local(down_ref, down_hbm, 16).wait()
+    local(ggain_ref, ggain_hbm, 17).wait()
 
 
 def layer(*args):
-    vm = pl.BlockSpec(memory_space=pltpu.VMEM)
     hbm = pl.BlockSpec(memory_space=pl.ANY)
     sem = pltpu.SemaphoreType.DMA
-    sems = [sem((12,))]
+    sems = [sem((20,))]
     for n in SEMS.values():
         sems += [sem((n,)), sem((n,))]
     out = jax.ShapeDtypeStruct
@@ -736,9 +769,15 @@
             out((FF_DP, ROWS_DP), BF),
             out((1, D), F32),
         ),
-        in_specs=[hbm] * 5 + [vm, vm, hbm, hbm, vm],
-        out_specs=(hbm,) * 4 + (vm,) * 3,
+        in_specs=[hbm] * 10,
+        out_specs=(hbm,) * 7,
         scratch_shapes=[
+            pltpu.VMEM((1, POS), jnp.int32),
+            pltpu.VMEM((1, 2, 2), jnp.int32),
+            pltpu.VMEM((1, ROWS_DP), BF),
+            pltpu.VMEM((ROWS_DP, FF_DP), BF),
+            pltpu.VMEM((FF_DP, ROWS_DP), BF),
+            pltpu.VMEM((1, D), F32),
             *[pltpu.VMEM((TOK, D), BF)] * 4,
             pltpu.VMEM((POS, D), BF),
             *[pltpu.VMEM((TOK, D), BF)] * 4,
@@ -783,37 +822,37 @@
 
 def hand_out_kernel(*refs):
     n = 7
-    ins, outs, held, taken, done = refs[:n], refs[n : 2 * n], refs[2 * n : -2], refs[-2], refs[-1]
-    into = [pltpu.make_async_copy(ins[i], held[i], taken.at[i]) for i in range(4)]
+    ins, outs, held = refs[:n], refs[n : 2 * n], refs[2 * n : 3 * n]
+    flat, taken, done = refs[3 * n :]
+    into = [pltpu.make_async_copy(ins[i], held[i], taken.at[i]) for i in range(n)]
     out = [
-        pltpu.make_async_copy(held[i] if i < 4 else ins[i], outs[i], done.at[i])
-        for i in range(n - 1)
+        pltpu.make_async_copy(held[i] if i < n - 1 else flat, outs[i], done.at[i])
+        for i in range(n)
     ]
     for copy in into:
         copy.start()
-    for copy in out[4:]:
-        copy.start()
-    outs[n - 1][...] = ins[n - 1][0, :]
-    for i in range(4):
+    for i in range(n):
         into[i].wait()
+        if i == n - 1:
+            flat[...] = held[i][0, :]
         out[i].start()
     for copy in out:
         copy.wait()
 
 
 def hand_out(arrays):
-    vm = pl.BlockSpec(memory_space=pltpu.VMEM)
     hbm = pl.BlockSpec(memory_space=pl.ANY)
     return pl.pallas_call(
         hand_out_kernel,
         out_shape=tuple(jax.ShapeDtypeStruct(a.shape, a.dtype) for a in arrays[:-1])
         + (jax.ShapeDtypeStruct((D,), F32),),
-        in_specs=[hbm] * 4 + [vm] * 3,
-        out_specs=(hbm,) * 6 + (vm,),
+        in_specs=[hbm] * 7,
+        out_specs=(hbm,) * 7,
         scratch_shapes=[
-            *[pltpu.VMEM((TOK, D), BF)] * 4,
-            pltpu.SemaphoreType.DMA((4,)),
-            pltpu.SemaphoreType.DMA((6,)),
+            *[pltpu.VMEM(a.shape, a.dtype) for a in arrays],
+            pltpu.VMEM((D,), F32),
+            pltpu.SemaphoreType.DMA((7,)),
+            pltpu.SemaphoreType.DMA((7,)),
         ],
     )(*arrays)
 

time: 95.8 us -> 104 us (1.086)
  Pallas kernels: 93.2 us -> 101 us
    pallas_call x1, Pallas kernels: 89.7 us -> 98.9 us  [layer(): pl.pallas_call(kernel, out_shape=(out((TOK, D), BF), out((TOK, D), BF), o...]
    pallas_call x1, Pallas kernels: 3.54 us -> 2.16 us  [hand_out(): pl.pallas_call(hand_out_kernel, out_shape=tuple((jax.ShapeDtypeStruct(a.s...]
where the time goes in v5:
time: 104 us; the launch traced here: 102 us
  Pallas kernels  101 us (97%)
    pallas_call x1, Pallas kernels, layer(): pl.pallas_call(kernel, out_shape=(out((TOK, D), BF), out((TOK, D), BF), o...  98.9 us
    pallas_call x1, Pallas kernels, hand_out(): pl.pallas_call(hand_out_kernel, out_shape=tuple((jax.ShapeDtypeStruct(a.s...  2.16 us

profile of v5, /device:TPU:31, one launch (start us, length us, event | category | flops | bytes accessed | tf_op | source)
XLA Modules:
  0.0 101.9 jit_solution(17189540405515614367)
XLA Ops:
  0.6 98.9 %shard_map.153 = (bf16[128,1280]{1,0:T(8,128)(2,1)}, bf16[128,1280]{1,0:T(8,128)(2,1)}, bf16[128,1280]{1,0:T(8,128)(2,1)}, bf16[128,1280]{1,0:T(8,128)(2,1)}, bf...) custom-call(bf16[128,1280]{1,0:T(8,128)(2,1)} %bitcast.11, bf16[128,1280]{1,0:T(8,128)(2,1)} %bitcast.12, ...), custom_call_target="tpu_custom_call" | custom-call | tf_op jit(solution)/shard_map/pallas_call | solution.py:761
  99.6 2.2 %shard_map.154 = (bf16[128,1280]{1,0:T(8,128)(2,1)}, bf16[128,1280]{1,0:T(8,128)(2,1)}, bf16[128,1280]{1,0:T(8,128)(2,1)}, bf16[128,1280]{1,0:T(8,128)(2,1)}, bf...) custom-call(bf16[128,1280]{1,0:T(8,128)(2,1)} %get-tuple-element.21.refs_0_, ...), custom_call_target="tpu_custom_call" | custom-call | tf_op jit(solution)/shard_map/pallas_call | solution.py:845

commit v6 on v3

--- a/solution.py
+++ b/solution.py
@@ -722,37 +722,37 @@
 
 def hand_out_kernel(*refs):
     n = 7
-    ins, outs, held, taken, done = refs[:n], refs[n : 2 * n], refs[2 * n : -2], refs[-2], refs[-1]
-    into = [pltpu.make_async_copy(ins[i], held[i], taken.at[i]) for i in range(4)]
+    ins, outs, held = refs[:n], refs[n : 2 * n], refs[2 * n : 3 * n]
+    flat, taken, done = refs[3 * n :]
+    into = [pltpu.make_async_copy(ins[i], held[i], taken.at[i]) for i in range(n)]
     out = [
-        pltpu.make_async_copy(held[i] if i < 4 else ins[i], outs[i], done.at[i])
-        for i in range(n - 1)
+        pltpu.make_async_copy(held[i] if i < n - 1 else flat, outs[i], done.at[i])
+        for i in range(n)
     ]
     for copy in into:
         copy.start()
-    for copy in out[4:]:
-        copy.start()
-    outs[n - 1][...] = ins[n - 1][0, :]
-    for i in range(4):
+    for i in range(n):
         into[i].wait()
+        if i == n - 1:
+            flat[...] = held[i][0, :]
         out[i].start()
     for copy in out:
         copy.wait()
 
 
 def hand_out(arrays):
-    vm = pl.BlockSpec(memory_space=pltpu.VMEM)
     hbm = pl.BlockSpec(memory_space=pl.ANY)
     return pl.pallas_call(
         hand_out_kernel,
         out_shape=tuple(jax.ShapeDtypeStruct(a.shape, a.dtype) for a in arrays[:-1])
         + (jax.ShapeDtypeStruct((D,), F32),),
-        in_specs=[hbm] * 4 + [vm] * 3,
-        out_specs=(hbm,) * 6 + (vm,),
+        in_specs=[hbm] * 7,
+        out_specs=(hbm,) * 7,
         scratch_shapes=[
-            *[pltpu.VMEM((TOK, D), BF)] * 4,
-            pltpu.SemaphoreType.DMA((4,)),
-            pltpu.SemaphoreType.DMA((6,)),
+            *[pltpu.VMEM(a.shape, a.dtype) for a in arrays],
+            pltpu.VMEM((D,), F32),
+            pltpu.SemaphoreType.DMA((7,)),
+            pltpu.SemaphoreType.DMA((7,)),
         ],
     )(*arrays)
 

time: 94.6 us -> 93.2 us (0.985)
  Pallas kernels: 93.5 us -> 92.1 us
    pallas_call x1, Pallas kernels: 3.54 us -> 2.16 us  [hand_out(): pl.pallas_call(hand_out_kernel, out_shape=tuple((jax.ShapeDtypeStruct(a.s...]
where the time goes in v6:
time: 93.2 us; the launch traced here: 92.9 us
  Pallas kernels  92.1 us (99%)
    pallas_call x1, Pallas kernels, layer(): pl.pallas_call(kernel, out_shape=(out((TOK, D), BF), out((TOK, D), BF), o...  89.9 us
    pallas_call x1, Pallas kernels, hand_out(): pl.pallas_call(hand_out_kernel, out_shape=tuple((jax.ShapeDtypeStruct(a.s...  2.16 us

profile of v6, /device:TPU:31, one launch (start us, length us, event | category | flops | bytes accessed | tf_op | source)
XLA Modules:
  0.0 92.9 jit_solution(1722711054822068040)
XLA Ops:
  0.6 89.9 %shard_map.153 = (bf16[128,1280]{1,0:T(8,128)(2,1)}, bf16[128,1280]{1,0:T(8,128)(2,1)}, bf16[128,1280]{1,0:T(8,128)(2,1)}, bf16[128,1280]{1,0:T(8,128)(2,1)}, bf...) custom-call(bf16[128,1280]{1,0:T(8,128)(2,1)} %bitcast.11, bf16[128,1280]{1,0:T(8,128)(2,1)} %bitcast.12, ...), custom_call_target="tpu_custom_call" | custom-call | tf_op jit(solution)/shard_map/pallas_call | solution.py:667
  90.6 2.2 %shard_map.154 = (bf16[128,1280]{1,0:T(8,128)(2,1)}, bf16[128,1280]{1,0:T(8,128)(2,1)}, bf16[128,1280]{1,0:T(8,128)(2,1)}, bf16[128,1280]{1,0:T(8,128)(2,1)}, bf...) custom-call(bf16[128,1280]{1,0:T(8,128)(2,1)} %get-tuple-element.21.refs_0_, ...), custom_call_target="tpu_custom_call" | custom-call | tf_op jit(solution)/shard_map/pallas_call | solution.py:745
